TPU v7x, 256 devices: a whole 4x4x8 slice. The times are simulated.
256 devices in a mesh: dom: 32 (over x, z), rows: 8 (over y, core).
Axes of the slice: x: 4, y: 4, z: 8, core: 2. Of those that a mesh axis runs over, the one named last changes fastest.
Arguments:
- features: bfloat16 [65536, 384], P(('dom', 'rows')), may hold values from -7 to 7
- out_grad: bfloat16 [65536, 384], P(('dom', 'rows')), may hold values from -6 to 6
- w_query: bfloat16 [384, 384], replicated, may hold values from -0.3125 to 0.3125
- w_keyval: bfloat16 [384, 768], replicated, may hold values from -0.3125 to 0.3125
- w_out: bfloat16 [384, 384], replicated, may hold values from -0.3125 to 0.3125
- virtual: bfloat16 [4, 384], replicated, may hold values from -6 to 6
- local_nbr: int32 [65536, 16], P(('dom', 'rows')), may hold values from 0 to 255
- expander: int32 [65536, 4], P(('dom', 'rows')), may hold values from 0 to 1023
- send_rows: int32 [8192, 32], P(('dom', 'rows')), may hold values from 0 to 255
Outputs:
- grad_features: float32 [65536, 384], P(('dom', 'rows'))
- grad_wq: float32 [384, 384], replicated
- grad_wkv: float32 [384, 768], replicated
- grad_wo: float32 [384, 384], replicated
- grad_virtual: float32 [4, 384], replicated
Inputs may be any that keep to these rules, and one draw needn't show every extreme that they name: `local_nbr`: positions 0 to 127 name the previous tile of the partition's block order (cyclic within the partition), 128 to 255 the node's own tile. `expander`: slot s * 32 + k of a device holds the k-th row that the device of dom index s and the same rows index sends to it. `send_rows`: row g * 32 + a lists the 32 local rows that device g sends to dom index a; every device sends exactly 32 rows to every dom index, itself included.
All inputs are finite; a program needn't handle non-finite values.
Results may differ from a plain program's by a relative error of at most 0.008.
The roundings to bfloat16 on the way count: a program that leaves them out, or rounds other values in their place, can miss the bound.
Values may be sent and summed in bfloat16 or wider, within the bound.
A program may use at most 64 MiB of HBM per device.

v0:
```python
import math

import jax
import jax.numpy as jnp
from jax import lax
from jax.sharding import PartitionSpec as P

HEADS = 8
TILE = 128


NEGATIVE_FILL = -1e30


def shifted(block, axis, distance):
    devices = range(lax.axis_size(axis))
    route = [((i - distance) % len(devices), i) for i in devices]
    return lax.ppermute(block, axis, route)


def einsum_bf(spec, left, right):
    return jnp.einsum(spec, left, right, preferred_element_type=jnp.float32)


def rows_contracted(left, right):
    return lax.dot_general(
        left, right, (((0,), (0,)), ((), ())), preferred_element_type=jnp.float32
    )


def times_transposed(left, right):
    return lax.dot_general(
        left, right, (((1,), (1,)), ((), ())), preferred_element_type=jnp.float32
    )


def attend(queries, key_value, halo_kv, expand_kv, virtual_kv, local_nbr, out_delta):
    row_count, feat_width = queries.shape
    head_count = HEADS
    head_dim = feat_width // head_count
    tile_rows = TILE
    tile_count = row_count // tile_rows
    score_scale = 1.0 / math.sqrt(head_dim)
    extended = jnp.concatenate([halo_kv, key_value], axis=0)
    window = jnp.concatenate(
        [
            extended[:row_count].reshape(tile_count, tile_rows, 2 * feat_width),
            key_value.reshape(tile_count, tile_rows, 2 * feat_width),
        ],
        axis=1,
    )
    win_keys = window[:, :, :feat_width].reshape(tile_count, 2 * tile_rows, head_count, head_dim)
    win_vals = window[:, :, feat_width:].reshape(tile_count, 2 * tile_rows, head_count, head_dim)
    exp_keys = expand_kv[:, :, :feat_width].reshape(row_count, -1, head_count, head_dim)
    exp_vals = expand_kv[:, :, feat_width:].reshape(row_count, -1, head_count, head_dim)
    virt_keys = virtual_kv[:, :feat_width].reshape(-1, head_count, head_dim)
    virt_vals = virtual_kv[:, feat_width:].reshape(-1, head_count, head_dim)
    q_heads = queries.reshape(row_count, head_count, head_dim)
    q_tiles = queries.reshape(tile_count, tile_rows, head_count, head_dim)
    d_heads = out_delta.reshape(row_count, head_count, head_dim)
    d_tiles = out_delta.reshape(tile_count, tile_rows, head_count, head_dim)
    positions = jnp.arange(2 * tile_rows, dtype=jnp.int32)
    local_mask = jnp.any(local_nbr[:, :, None] == positions[None, None, :], axis=1)[:, None, :]
    s_loc = (
        einsum_bf("tqhd,tkhd->tqhk", q_tiles, win_keys).reshape(
            row_count, head_count, 2 * tile_rows
        )
        * score_scale
    )
    s_loc = jnp.where(local_mask, s_loc, NEGATIVE_FILL)
    s_exp = einsum_bf("rhd,rkhd->rhk", q_heads, exp_keys) * score_scale
    s_virt = einsum_bf("rhd,khd->rhk", q_heads, virt_keys) * score_scale
    row_peak = jnp.maximum(jnp.maximum(s_loc.max(-1), s_exp.max(-1)), s_virt.max(-1))[..., None]
    e_loc = jnp.where(local_mask, jnp.exp(s_loc - row_peak), 0.0)
    e_exp = jnp.exp(s_exp - row_peak)
    e_virt = jnp.exp(s_virt - row_peak)
    norm_total = (e_loc.sum(-1) + e_exp.sum(-1) + e_virt.sum(-1))[..., None]
    p_loc = e_loc / norm_total
    p_exp = e_exp / norm_total
    p_virt = e_virt / norm_total
    pb_loc = p_loc.astype(jnp.bfloat16)
    pb_exp = p_exp.astype(jnp.bfloat16)
    pb_virt = p_virt.astype(jnp.bfloat16)
    pb_tiles = pb_loc.reshape(tile_count, tile_rows, head_count, 2 * tile_rows)
    summed = (
        einsum_bf("tqhk,tkhd->tqhd", pb_tiles, win_vals).reshape(row_count, feat_width)
        + einsum_bf("rhk,rkhd->rhd", pb_exp, exp_vals).reshape(row_count, feat_width)
        + einsum_bf("rhk,khd->rhd", pb_virt, virt_vals).reshape(row_count, feat_width)
    )
    attn_out = summed.astype(jnp.bfloat16)
    dp_loc = einsum_bf("tqhd,tkhd->tqhk", d_tiles, win_vals).reshape(
        row_count, head_count, 2 * tile_rows
    )
    dp_exp = einsum_bf("rhd,rkhd->rhk", d_heads, exp_vals)
    dp_virt = einsum_bf("rhd,khd->rhk", d_heads, virt_vals)
    delta = ((p_loc * dp_loc).sum(-1) + (p_exp * dp_exp).sum(-1) + (p_virt * dp_virt).sum(-1))[
        ..., None
    ]
    ds_loc = (p_loc * (dp_loc - delta) * score_scale).astype(jnp.bfloat16)
    ds_exp = (p_exp * (dp_exp - delta) * score_scale).astype(jnp.bfloat16)
    ds_virt = (p_virt * (dp_virt - delta) * score_scale).astype(jnp.bfloat16)
    ds_tiles = ds_loc.reshape(tile_count, tile_rows, head_count, 2 * tile_rows)
    grad_query = (
        einsum_bf("tqhk,tkhd->tqhd", ds_tiles, win_keys).reshape(row_count, feat_width)
        + einsum_bf("rhk,rkhd->rhd", ds_exp, exp_keys).reshape(row_count, feat_width)
        + einsum_bf("rhk,khd->rhd", ds_virt, virt_keys).reshape(row_count, feat_width)
    ).astype(jnp.bfloat16)
    win_kgrad = einsum_bf("tqhk,tqhd->tkhd", ds_tiles, q_tiles).reshape(
        tile_count, 2 * tile_rows, feat_width
    )
    win_vgrad = einsum_bf("tqhk,tqhd->tkhd", pb_tiles, d_tiles).reshape(
        tile_count, 2 * tile_rows, feat_width
    )
    window_grad = jnp.concatenate([win_kgrad, win_vgrad], axis=-1)
    exp_grad = jnp.concatenate(
        [
            einsum_bf("rhk,rhd->rkhd", ds_exp, q_heads).reshape(row_count, -1, feat_width),
            einsum_bf("rhk,rhd->rkhd", pb_exp, d_heads).reshape(row_count, -1, feat_width),
        ],
        axis=-1,
    )
    virt_grad = jnp.concatenate(
        [
            einsum_bf("rhk,rhd->khd", ds_virt, q_heads).reshape(-1, feat_width),
            einsum_bf("rhk,rhd->khd", pb_virt, d_heads).reshape(-1, feat_width),
        ],
        axis=-1,
    )
    return (attn_out, grad_query, window_grad, exp_grad, virt_grad)


def project_slots(slot_grad, w_keyval):
    return lax.optimization_barrier(times_transposed(slot_grad, w_keyval).astype(jnp.bfloat16))


def shards(features, out_grad, w_query, w_keyval, w_out, virtual, local_nbr, expander, send_rows):
    row_count, feat_width = features.shape
    tile_rows = TILE
    queries = jnp.dot(features, w_query, preferred_element_type=jnp.float32).astype(jnp.bfloat16)
    key_value = jnp.dot(features, w_keyval, preferred_element_type=jnp.float32).astype(jnp.bfloat16)
    virtual_kv = jnp.dot(virtual, w_keyval, preferred_element_type=jnp.float32).astype(jnp.bfloat16)
    send_flat = send_rows.reshape(-1)
    sent_features = features[send_flat]
    halo_kv = shifted(key_value[row_count - tile_rows :], "rows", 1)
    slot_kv = lax.all_to_all(key_value[send_flat], "dom", split_axis=0, concat_axis=0, tiled=True)
    expand_kv = slot_kv[expander]
    out_delta = times_transposed(out_grad, w_out).astype(jnp.bfloat16)
    attn_out, grad_query, window_grad, exp_grad, virt_grad = attend(
        queries, key_value, halo_kv, expand_kv, virtual_kv, local_nbr, out_delta
    )
    own_grad = window_grad[:, tile_rows:].reshape(row_count, 2 * feat_width)
    prev_grad = window_grad[:, :tile_rows].reshape(row_count, 2 * feat_width)
    returned = shifted(prev_grad[:tile_rows].astype(jnp.bfloat16), "rows", -1).astype(jnp.float32)
    local_grad = (own_grad + jnp.concatenate([prev_grad[tile_rows:], returned], axis=0)).astype(
        jnp.bfloat16
    )
    slot_grad = jax.ops.segment_sum(
        exp_grad.reshape(-1, 2 * feat_width), expander.reshape(-1), num_segments=slot_kv.shape[0]
    ).astype(jnp.bfloat16)
    returned_slots = lax.all_to_all(slot_grad, "dom", split_axis=0, concat_axis=0, tiled=True)
    returned_feat = project_slots(returned_slots, w_keyval)
    slot_weight = rows_contracted(sent_features, returned_slots)
    grad_features = times_transposed(grad_query, w_query) + times_transposed(local_grad, w_keyval)
    grad_features = grad_features.at[send_flat].add(returned_feat.astype(jnp.float32))
    grad_wq, grad_wkv, grad_wo, virt_total = lax.psum(
        (
            rows_contracted(features, grad_query),
            rows_contracted(features, local_grad) + slot_weight,
            rows_contracted(attn_out, out_grad),
            virt_grad,
        ),
        ("dom", "rows"),
    )
    grad_wkv = grad_wkv + jnp.dot(
        virtual.astype(jnp.float32).T, virt_total, precision=lax.Precision.HIGHEST
    )
    grad_virtual = jnp.dot(
        virt_total, w_keyval.astype(jnp.float32).T, precision=lax.Precision.HIGHEST
    )
    factor = (row_count * lax.axis_size("dom") * lax.axis_size("rows")) ** (-0.5)
    return (
        grad_features,
        grad_wq * factor,
        grad_wkv * factor,
        grad_wo * factor,
        grad_virtual * factor,
    )


def solution(mesh):
    placed = (
        P(("dom", "rows"), None),
        P(("dom", "rows"), None),
        P(),
        P(),
        P(),
        P(),
        P(("dom", "rows"), None),
        P(("dom", "rows"), None),
        P(("dom", "rows"), None),
    )
    return jax.shard_map(
        shards,
        mesh=mesh,
        in_specs=placed,
        out_specs=(P(("dom", "rows"), None), P(), P(), P(), P()),
        check_vma=False,
    )
```

profile of v0, /device:TPU:1, one launch (start us, length us, event | category | flops | bytes accessed | tf_op | source)
XLA Modules:
  0.0 454.2 jit_solution(4972077275329131479)
XLA Ops:
  9.6 5.2 %gather_fusion = bf16[1024,768]{1,0:T(8,128)(2,1)} fusion(bf16[256,768]{1,0:T(8,128)(2,1)S(1)} %convolution_convert_fusion.1, s32[1024]{0:T(1024)S(1)} %broadcast_clamp_fusion.1), kind=kCustom, calls=%fused_computation | custom fusion | bytes 3149824 | tf_op jit(solution)/shard_map/gather | solution.py:145
  14.8 12.0 %all-to-all-start = ((bf16[32,32,768]{2,1,0:T(8,128)(2,1)}), bf16[32,32,768]{2,1,0:T(8,128)(2,1)S(1)}, u32[]{:S(2)}, u32[]{:S(2)}) async-start(bf16[32,32,768]{2,1,0:T(8,128)(2,1)} %bitcast.221), calls=%async_computation | async-start | bytes 3145728 | tf_op jit(solution)/shard_map/all_to_all | solution.py:145
  27.5 2.1 collective-permute-start
  29.6 5.0 %gather_fusion.2 = bf16[1024,384]{1,0:T(8,128)(2,1)} fusion(bf16[256,384]{1,0:T(8,128)(2,1)S(1)} %copy-done.1, s32[1024]{0:T(1024)S(1)} %broadcast_clamp_fusion.1), kind=kCustom, calls=%fused_computation.2 | custom fusion | bytes 1576960 | tf_op jit(solution)/shard_map/gather | solution.py:143
  43.5 1.6 fusion
  50.5 1.9 copy.88
  52.4 2.8 fusion.9
  55.2 8.5 %all-to-all-done = bf16[32,32,768]{2,1,0:T(8,128)(2,1)S(1)} async-done(((bf16[32,32,768]{2,1,0:T(8,128)(2,1)}), bf16[32,32,768]{2,1,0:T(8,128)(2,1)S(1)}, u32[]{:S(2)}, u32[]{:S(2)}) %all-to-all-start) | async-done | bytes 1572896 | tf_op jit(solution)/shard_map/all_to_all | solution.py:145
  63.7 5.2 %gather_fusion.1 = bf16[1024,768]{1,0:T(8,128)(2,1)} fusion(bf16[1024,768]{1,0:T(8,128)(2,1)S(1)} %bitcast.205, s32[1024]{0:T(1024)S(1)} %broadcast_clamp_fusion), kind=kCustom, calls=%fused_computation.1 | custom fusion | bytes 3149824 | tf_op jit(solution)/shard_map/gather | solution.py:146
  68.9 2.9 reshape.232
  71.8 1.7 fusion.62
  73.5 2.4 copy.149
  75.9 1.5 multiply_reduce_fusion.3
  81.3 1.8 copy.106
  83.1 2.2 copy.150
  85.3 2.6 convolution_bitcast_fusion.3
  94.1 1.8 copy.104
  95.9 2.1 copy.111
  99.1 4.0 multiply_bitcast_fusion.1
  103.1 4.6 %concatenate.27 = f32[1024,384]{1,0:T(8,128)} reshape(f32[256,4,8,48]{3,2,1,0:T(8,128)} %multiply_bitcast_fusion.1) | data formatting | bytes 3145728 | tf_op jit(solution)/shard_map/concatenate | solution.py:115
  107.7 4.5 %multiply_bitcast_fusion = f32[256,4,8,48]{3,2,1,0:T(8,128)} fusion(f32[256,8,4]{1,2,0:T(4,128)} %copy.106, f32[256,8,48]{2,1,0:T(8,128)} %copy.105), kind=kLoop, calls=%fused_computation.5 | loop fusion | flops 393216 | bytes 1998848 | tf_op jit(solution)/shard_map/rhk,rhd->rkhd/transpose | solution.py:22
  112.2 4.6 %concatenate.28 = f32[1024,384]{1,0:T(8,128)} reshape(f32[256,4,8,48]{3,2,1,0:T(8,128)} %multiply_bitcast_fusion) | data formatting | bytes 3145728 | tf_op jit(solution)/shard_map/concatenate | solution.py:115
  116.8 9.9 %scatter_custom_fusion = f32[1024,768]{1,0:T(8,128)} fusion(s32[1024]{0:T(1024)} %reshape.249, f32[1024,384]{1,0:T(8,128)} %concatenate.28, f32[]{:T(128)} %constant.12.clone.1, f32[1024,384]{1,0:T(8,128)} %concatenate.27, f32[]{:T(128)} %constant.2.clone.1), kind=kCustom, calls=%fused_computation.9 | custom fusion | flops 1572864 | bytes 6292480 | tf_op jit(solution)/shard_map/scatter-add | solution.py:157
  126.7 3.2 convert_element_type.72
  130.0 7.8 %all-to-all-start.1 = ((bf16[32,32,768]{2,1,0:T(8,128)(2,1)}), bf16[32,32,768]{2,1,0:T(8,128)(2,1)}, u32[]{:S(2)}, u32[]{:S(2)}) async-start(bf16[32,32,768]{2,1,0:T(8,128)(2,1)} %bitcast.220), calls=%async_computation.1 | async-start | bytes 3145728 | tf_op jit(solution)/shard_map/all_to_all | solution.py:160
  139.0 1.5 collective-permute-start.1
  146.0 28.7 %all-to-all-done.1 = bf16[32,32,768]{2,1,0:T(8,128)(2,1)} async-done(((bf16[32,32,768]{2,1,0:T(8,128)(2,1)}), bf16[32,32,768]{2,1,0:T(8,128)(2,1)}, u32[]{:S(2)}, u32[]{:S(2)}) %all-to-all-start.1) | async-done | bytes 1572896 | tf_op jit(solution)/shard_map/all_to_all | solution.py:160
  174.7 3.7 convolution_add_fusion
  178.7 78.5 %psum.30 = f32[4,768]{1,0:T(4,128)S(1)} all-reduce(f32[4,768]{1,0:T(4,128)S(1)} %pad_maximum_fusion.3), channel_id=1, replica_groups=mesh['dom'=32,'rows'=8] {'dom','rows'}, use_global_device_ids=true, to_apply=%region_14.15 | all-reduce | flops 3072 | bytes 24576 | tf_op jit(solution)/shard_map/psum | solution.py:165
  259.2 2.4 convolution_convert_fusion
  261.6 7.0 %scatter_custom_fusion.1 = f32[256,384]{1,0:T(8,128)S(1)} fusion(f32[256,384]{1,0:T(8,128)S(1)} %convolution_add_fusion.1, s32[1024]{0:T(1024)} %bitcast.235, bf16[1024,384]{1,0:T(8,128)(2,1)S(1)} %convolution_convert_fusion), kind=kCustom, calls=%fused_computation.30 | custom fusion | flops 786432 | bytes 1179648 | tf_op jit(solution)/shard_map/scatter-add | solution.py:164
  268.6 173.0 %all-reduce.3.cloned.1.call-done = (f32[384,384]{0,1:T(8,128)}, f32[384,768]{0,1:T(8,128)}, f32[384,384]{0,1:T(8,128)}) async-done(((f32[384,384]{0,1:T(8,128)}, f32[384,768]{0,1:T(8,128)}, f32[384,384]{0,1:T(8,128)}), (f32[384,384]{0,1:T(8,128)}, f32[384,768]{0,1:T(8,128)}, f32[384,384]{0,1:T(8,128)})) %all-reduce.3.cloned.1.call-update) | async-done | bytes 2359312 | tf_op jit(solution)/shard_map/psum | solution.py:165
  (192 shorter events, 42.7 us)
Async XLA Ops:
  14.8 14.8 %copy-start.1 = (bf16[256,384]{1,0:T(8,128)(2,1)S(1)}, bf16[256,384]{1,0:T(8,128)(2,1)}, u32[]{:S(2)}) copy-start(bf16[256,384]{1,0:T(8,128)(2,1)} %param.9) | copy-start | bytes 589828
  14.8 48.9 %all-to-all-start = ((bf16[32,32,768]{2,1,0:T(8,128)(2,1)}), bf16[32,32,768]{2,1,0:T(8,128)(2,1)S(1)}, u32[]{:S(2)}, u32[]{:S(2)}) async-start(bf16[32,32,768]{2,1,0:T(8,128)(2,1)} %bitcast.221), calls=%async_computation | async-start | bytes 3145728 | tf_op jit(solution)/shard_map/all_to_all | solution.py:145
  27.5 7.1 %copy-start.17 = (bf16[384,384]{1,0:T(8,128)(2,1)S(1)}, bf16[384,384]{1,0:T(8,128)(2,1)}, u32[]{:S(2)}) copy-start(bf16[384,384]{1,0:T(8,128)(2,1)} %param.11) | copy-start | bytes 884740
  27.5 19.9 %collective-permute-start = (bf16[128,768]{1,0:T(8,128)(2,1)}, bf16[128,768]{1,0:T(8,128)(2,1)}, u32[]{:S(2)}, u32[]{:S(2)}) collective-permute-start(bf16[128,768]{1,0:T(8,128)(2,1)} %slice.59), channel_id=1, source_target_pairs={{7,0},{0,1},{1,2},{2,3},{3,4},{4,5},{5,6},{6,7},{15,8},{8,9},{9,10... | collective-permute-start | bytes 589832 | tf_op jit(solution)/shard_map/ppermute | solution.py:18
  36.5 5.5 %copy-start.52 = (bf16[4,384]{1,0:T(4,128)(2,1)S(1)}, bf16[4,384]{1,0:T(4,128)(2,1)}, u32[]{:S(2)}) copy-start(bf16[4,384]{1,0:T(4,128)(2,1)} %param.14) | copy-start | bytes 9220
  37.8 5.3 %copy-start.50 = (s32[256,4]{0,1:T(4,128)S(1)}, s32[256,4]{0,1:T(4,128)}, u32[]{:S(2)}) copy-start(s32[256,4]{0,1:T(4,128)} %param.16) | copy-start | bytes 12292
  37.8 5.7 %copy-start.49 = (s32[256,16]{0,1:T(8,128)S(1)}, s32[256,16]{0,1:T(8,128)}, u32[]{:S(2)}) copy-start(s32[256,16]{0,1:T(8,128)} %param.15) | copy-start | bytes 49156
  39.3 9.1 %copy-start.8 = (bf16[256,384]{0,1:T(8,128)(2,1)}, bf16[256,384]{0,1:T(8,128)(2,1)S(1)}, u32[]{:S(2)}) copy-start(bf16[256,384]{0,1:T(8,128)(2,1)S(1)} %copy.89) | copy-start | bytes 589828
  42.3 8.2 %copy-start.40 = (bf16[4,8,48]{2,1,0:T(8,128)(2,1)}, bf16[4,8,48]{2,1,0:T(8,128)(2,1)S(1)}, u32[]{:S(2)}) copy-start(bf16[4,8,48]{2,1,0:T(8,128)(2,1)S(1)} %reshape.206) | copy-start | bytes 9220
  73.5 3.9 copy-start.42
  73.5 4.7 %copy-start.2 = (f32[2,8,256,128]{3,2,1,0:T(8,128)S(1)}, f32[2,8,256,128]{3,2,1,0:T(8,128)}, u32[]{:S(2)}) copy-start(f32[2,8,256,128]{3,2,1,0:T(8,128)} %get-tuple-element.39) | copy-start | bytes 6291460
  75.9 2.8 copy-start.20
  75.9 2.9 copy-start.9
  75.9 2.9 copy-start.43
  77.4 2.7 copy-start.28
  78.1 11.3 %copy-start.35 = (f32[2,128,8]{1,2,0:T(8,128)}, f32[2,128,8]{1,2,0:T(8,128)S(1)}, u32[]{:S(2)}) copy-start(f32[2,128,8]{1,2,0:T(8,128)S(1)} %bitcast_maximum_fusion.1) | copy-start | bytes 24580
  78.8 10.7 %copy-start.45 = (f32[2,128,8]{1,2,0:T(8,128)}, f32[2,128,8]{1,2,0:T(8,128)S(1)}, u32[]{:S(2)}) copy-start(f32[2,128,8]{1,2,0:T(8,128)S(1)} %bitcast_add_fusion.7) | copy-start | bytes 24580
  85.3 2.6 copy-start.23
  85.3 2.6 copy-start.26
  90.4 2.5 copy-start.21
  91.5 6.6 %copy-start.12 = (f32[2,128,8,48]{1,3,2,0:T(8,128)S(1)}, f32[2,128,8,48]{1,3,2,0:T(8,128)}, u32[]{:S(2)}) copy-start(f32[2,128,8,48]{1,3,2,0:T(8,128)} %convolution_bitcast_fusion.4) | copy-start | bytes 1179652
  95.9 3.2 copy-start.7
  129.9 7.8 %copy-start.27 = (bf16[2,128,8,48]{1,0,3,2:T(2,128)(2,1)S(1)}, bf16[2,128,8,48]{1,0,3,2:T(2,128)(2,1)}, u32[]{:S(2)}) copy-start(bf16[2,128,8,48]{1,0,3,2:T(2,128)(2,1)} %reshape.208) | copy-start | bytes 589828
  130.0 7.9 %copy-start.36 = (f32[2,128,8]{1,2,0:T(8,128)S(1)}, f32[2,128,8]{1,2,0:T(8,128)}, u32[]{:S(2)}) copy-start(f32[2,128,8]{1,2,0:T(8,128)} %copy-done.35) | copy-start | bytes 24580
  130.0 7.9 %copy-start.46 = (f32[2,128,8]{1,2,0:T(8,128)S(1)}, f32[2,128,8]{1,2,0:T(8,128)}, u32[]{:S(2)}) copy-start(f32[2,128,8]{1,2,0:T(8,128)} %copy-done.45) | copy-start | bytes 24580
  130.0 44.7 %all-to-all-start.1 = ((bf16[32,32,768]{2,1,0:T(8,128)(2,1)}), bf16[32,32,768]{2,1,0:T(8,128)(2,1)}, u32[]{:S(2)}, u32[]{:S(2)}) async-start(bf16[32,32,768]{2,1,0:T(8,128)(2,1)} %bitcast.220), calls=%async_computation.1 | async-start | bytes 3145728 | tf_op jit(solution)/shard_map/all_to_all | solution.py:160
  137.7 303.8 %all-reduce.3.cloned.1.call-start = ((), (), s32[]{:S(2)}) async-start(), calls=%async_computation.2 | async-start | bytes 4718592 | tf_op jit(solution)/shard_map/psum | solution.py:165
  139.0 6.4 %collective-permute-start.1 = (bf16[128,768]{0,1:T(8,128)(2,1)S(1)}, bf16[128,768]{0,1:T(8,128)(2,1)S(1)}, u32[]{:S(2)}, u32[]{:S(2)}) collective-permute-start(bf16[128,768]{0,1:T(8,128)(2,1)S(1)} %fusion.32), channel_id=1, source_target_pairs={{1,0},{2,1},{3,2},{4,3},{5,4},{6,5},{7,6},{0,7},{9,8},{10,9},{11,1... | collective-permute-start | bytes 589832 | tf_op jit(solution)/shard_map/ppermute | solution.py:18
  178.4 80.5 %copy-start.18 = (bf16[384,384]{1,0:T(8,128)(2,1)S(1)}, bf16[384,384]{1,0:T(8,128)(2,1)}, u32[]{:S(2)}) copy-start(bf16[384,384]{1,0:T(8,128)(2,1)} %param.11) | copy-start | bytes 884740
  268.6 176.5 %copy-start.24 = (f32[256,384]{1,0:T(8,128)}, f32[256,384]{1,0:T(8,128)S(1)}, u32[]{:S(2)}) copy-start(f32[256,384]{1,0:T(8,128)S(1)} %scatter_custom_fusion.1) | copy-start | bytes 1179652
  441.6 3.5 copy-start.16
  441.6 3.5 copy-start.53
  (27 other events, 45.7 us)
Sparse Core Ops, SparseCore 0:
  178.5 263.0 all-reduce.2
where the time goes:
time: 456 us; the launch traced here: 454 us
  waiting for transfers between devices  212 us (46%)
  blocking collectives  78.5 us (17%)
  local copies, waits for them, and re-layouts  58.6 us (13%)
  other arithmetic  39.9 us (9%)
  matrix products  27.4 us (6%)
  starting transfers between devices  23.4 us (5%)
  between operations  14.8 us (3%)
    psum x1, waiting for transfers between devices, shards(): lax.psum((rows_contracted(features, grad_query), rows_contracted(features...  173 us
    psum x1, blocking collectives, shards(): lax.psum((rows_contracted(features, grad_query), rows_contracted(features...  78.5 us
    all_to_all x1, waiting for transfers between devices, shards(): lax.all_to_all(slot_grad, 'dom', split_axis=0, concat_axis=0, tiled=True)  28.7 us
    dot_general x12, matrix products, einsum_bf(): return jnp.einsum(spec, left, right, preferred_element_type=jnp.float32)  12.9 us
    all_to_all x1, starting transfers between devices, shards(): lax.all_to_all(key_value[send_flat], 'dom', split_axis=0, concat_axis=0,...  12 us
    unnamed x117, local copies, waits for them, and re-layouts  11.8 us
    scatter-add x1, other arithmetic, shards(): jax.ops.segment_sum(exp_grad.reshape(-1, 2 * feat_width), expander.reshap...  9.95 us
    concatenate x2, local copies, waits for them, and re-layouts, attend(): jnp.concatenate([einsum_bf('rhk,rhd->rkhd', ds_exp, q_heads).reshape(row_...  9.14 us
  transfers between devices with their start and end apart: 5, of which 4 were waited for; matrix products, arithmetic and copies ran while one was open for 9% of the time, Pallas kernels for 0%

commit v1 on v0

v1 whole, which is shorter than its diff:
```python
import functools
import math

import jax
import jax.numpy as jnp
from jax import lax
from jax.experimental import pallas as pl
from jax.experimental.pallas import tpu as pltpu
from jax.sharding import PartitionSpec as P

HEADS = 8
TILE = 128
LANES = 128
VROWS = 16
NEGATIVE_FILL = -1e30

F32 = jnp.float32
BF16 = jnp.bfloat16
VMEM = pl.BlockSpec(memory_space=pltpu.VMEM)


def contract(left, right, left_dim, right_dim):
    return lax.dot_general(
        left, right, (((left_dim,), (right_dim,)), ((), ())), preferred_element_type=F32
    )


def row_picker(send_flat, row_count):
    rows = lax.broadcasted_iota(jnp.int32, (row_count, send_flat.shape[1]), 0)
    return (rows == send_flat).astype(F32).astype(BF16)


def remote(src, dst, send_sem, recv_sem, dom, row):
    return pltpu.make_async_remote_copy(
        src_ref=src,
        dst_ref=dst,
        send_sem=send_sem,
        recv_sem=recv_sem,
        device_id=(dom, row),
        device_id_type=pl.DeviceIdType.MESH,
    )


def greet(n_dom, n_rows):
    dom, row = lax.axis_index("dom"), lax.axis_index("rows")
    barrier = pltpu.get_barrier_semaphore()

    def dom_peer(step, carry):
        pl.semaphore_signal(
            barrier,
            inc=1,
            device_id=(lax.rem(dom + step, n_dom), row),
            device_id_type=pl.DeviceIdType.MESH,
        )
        return carry

    def row_peer(step, carry):
        pl.semaphore_signal(
            barrier,
            inc=1,
            device_id=(dom, lax.rem(row + step, n_rows)),
            device_id_type=pl.DeviceIdType.MESH,
        )
        return carry

    lax.fori_loop(1, n_dom, dom_peer, 0)
    lax.fori_loop(1, n_rows, row_peer, 0)
    return barrier, n_dom + n_rows - 2


def spread_kernel(
    n_dom, n_rows, send_flat, feat, slots, halo, picked, send_sem, recv_sem, halo_send, halo_recv
):
    dom, row = lax.axis_index("dom"), lax.axis_index("rows")
    barrier, arrivals = greet(n_dom, n_rows)
    row_count, width = feat.shape
    picker = row_picker(send_flat[...], row_count)
    picked[...] = contract(picker, feat[...], 0, 0).astype(BF16).reshape(picked.shape)
    pl.semaphore_wait(barrier, arrivals)

    following = lax.rem(row + 1, n_rows)
    halo_copy = remote(
        feat.at[pl.ds(row_count - TILE, TILE)], halo, halo_send, halo_recv, dom, following
    )
    halo_copy.start()

    def copy_of(step):
        peer = lax.rem(dom + step, n_dom)
        return remote(
            picked.at[peer], slots.at[dom], send_sem.at[step], recv_sem.at[step], peer, row
        )

    def start(step, carry):
        copy_of(step).start()
        return carry

    def finish(step, carry):
        copy_of(step).wait()
        return carry

    lax.fori_loop(1, n_dom, start, 0)
    slots[dom] = picked[dom]
    halo_copy.wait()
    lax.fori_loop(1, n_dom, finish, 0)


def attend_kernel(
    feat,
    halo,
    slotf,
    out_grad,
    w_query,
    w_keyval,
    w_out,
    virt,
    local_nbr,
    expander,
    slot_feat,
    halo_feat,
    weight_sums,
    virt_feat,
    grad_feat,
    ext,
    q_t,
    d_t,
    kv_t,
    slot_kv,
    named,
    edge_kv,
    bias,
    edge_s,
    edge_dp,
    edge_p,
    edge_ds,
    kv_grad,
    out_t,
    dq_t,
    edge_grad,
):
    row_count, width = feat.shape
    slot_count = slotf.shape[0]
    head_dim = width // HEADS
    degree = expander.shape[0]
    scale = 1.0 / math.sqrt(head_dim)
    tiles = row_count // TILE

    ext[0:TILE] = halo[...]
    ext[TILE:] = feat[...]
    q_t[...] = contract(w_query[...], feat[...], 0, 1).astype(BF16)
    d_t[...] = contract(w_out[...], out_grad[...], 1, 1).astype(BF16)
    kv_t[...] = contract(w_keyval[...], ext[...], 0, 1).astype(BF16)
    virt_kv = contract(w_keyval[...], virt[...], 0, 1).astype(BF16).astype(F32)
    slot_kv[...] = contract(w_keyval[...], slotf[...], 0, 1).astype(BF16)

    positions = lax.broadcasted_iota(jnp.int32, (2 * TILE, row_count), 0)
    mask = positions == local_nbr[0:1, :]
    for entry in range(1, local_nbr.shape[0]):
        mask = jnp.logical_or(mask, positions == local_nbr[entry : entry + 1, :])
    bias[...] = jnp.where(mask, 0.0, NEGATIVE_FILL)

    slot_ids = lax.broadcasted_iota(jnp.int32, (slot_count, row_count), 0)
    q_wide = q_t[...].astype(F32)
    d_wide = d_t[...].astype(F32)

    def per_head(product):
        return product.reshape(HEADS, head_dim, row_count).sum(axis=1)

    def virtual_edge(v):
        return jnp.broadcast_to(virt_kv[:, v : v + 1], (2 * width, row_count))

    for k in range(degree):
        hot = (slot_ids == expander[k : k + 1, :]).astype(F32).astype(BF16)
        named[:, k * row_count : (k + 1) * row_count] = hot
        edge_kv[k] = contract(slot_kv[...], hot, 1, 0).astype(BF16)
        edge_s[:, k, :] = per_head(q_wide * edge_kv[k, 0:width].astype(F32)) * scale
        edge_dp[:, k, :] = per_head(d_wide * edge_kv[k, width:].astype(F32))
    for v in range(4):
        both = virtual_edge(v)
        edge_s[:, degree + v, :] = per_head(q_wide * both[0:width]) * scale
        edge_dp[:, degree + v, :] = per_head(d_wide * both[width:])

    kv_grad[...] = jnp.zeros_like(kv_grad)
    for h in range(HEADS):
        own = slice(h * head_dim, (h + 1) * head_dim)
        val = slice(width + h * head_dim, width + (h + 1) * head_dim)
        for t in range(tiles):
            here = slice(t * TILE, (t + 1) * TILE)
            window = slice(t * TILE, (t + 2) * TILE)
            keys, values = kv_t[own, window], kv_t[val, window]
            q_h, d_h = q_t[own, here], d_t[own, here]
            s = contract(keys, q_h, 0, 0) * scale + bias[:, here]
            se = edge_s[h, :, here]
            peak = jnp.maximum(
                jnp.max(s, axis=0, keepdims=True), jnp.max(se, axis=0, keepdims=True)
            )
            e = jnp.exp(s - peak)
            ee = jnp.exp(se - peak)
            inverse = 1.0 / (
                jnp.sum(e, axis=0, keepdims=True) + jnp.sum(ee, axis=0, keepdims=True)
            )
            p = e * inverse
            pe = ee * inverse
            dp = contract(values, d_h, 0, 0)
            dpe = edge_dp[h, :, here]
            delta = jnp.sum(p * dp, axis=0, keepdims=True) + jnp.sum(
                pe * dpe, axis=0, keepdims=True
            )
            ds = (p * (dp - delta) * scale).astype(BF16)
            pb = p.astype(BF16)
            edge_p[h, :, here] = pe.astype(BF16).astype(F32)
            edge_ds[h, :, here] = (pe * (dpe - delta) * scale).astype(BF16).astype(F32)
            out_t[own, here] = contract(values, pb, 1, 0)
            dq_t[own, here] = contract(keys, ds, 1, 0)
            kv_grad[own, window] += contract(q_h, ds, 1, 1)
            kv_grad[val, window] += contract(d_h, pb, 1, 1)

    def widen(rows):
        return jnp.broadcast_to(rows[:, None, :], (HEADS, head_dim, row_count)).reshape(
            width, row_count
        )

    out_sum = out_t[...]
    dq_sum = dq_t[...]
    lane = lax.broadcasted_iota(jnp.int32, (2 * width, LANES), 1)
    virt_t = jnp.zeros((2 * width, LANES), F32)
    for k in range(degree + 4):
        pk, dsk = widen(edge_p[:, k, :]), widen(edge_ds[:, k, :])
        if k < degree:
            key_k, val_k = edge_kv[k, 0:width].astype(F32), edge_kv[k, width:].astype(F32)
        else:
            both = virtual_edge(k - degree)
            key_k, val_k = both[0:width], both[width:]
        out_sum = out_sum + pk * val_k
        dq_sum = dq_sum + dsk * key_k
        to_key, to_val = dsk * q_wide, pk * d_wide
        if k < degree:
            cols = slice(k * row_count, (k + 1) * row_count)
            edge_grad[0:width, cols] = to_key.astype(BF16)
            edge_grad[width:, cols] = to_val.astype(BF16)
        else:
            column = jnp.concatenate(
                [jnp.sum(to_key, axis=1, keepdims=True), jnp.sum(to_val, axis=1, keepdims=True)],
                axis=0,
            )
            virt_t = jnp.where(lane == k - degree, column, virt_t)
    out_b = out_sum.astype(BF16)
    dq_b = dq_sum.astype(BF16)

    slot_grad = contract(edge_grad[...], named[...], 1, 1).astype(BF16)
    slot_feat[...] = contract(slot_grad, w_keyval[...], 0, 1).astype(BF16)
    halo_feat[...] = contract(
        kv_grad[:, 0:TILE].astype(BF16), w_keyval[...], 0, 1
    ).astype(BF16)
    own_grad = kv_grad[:, TILE:].astype(BF16)
    grad_feat[...] = contract(w_query[...], dq_b, 1, 0) + contract(
        w_keyval[...], own_grad, 1, 0
    )
    virt_hi = virt_t.astype(BF16)
    virt_lo = (virt_t - virt_hi.astype(F32)).astype(BF16)
    virt_feat[...] = (
        contract(virt_hi, w_keyval[...], 0, 1) + contract(virt_lo, w_keyval[...], 0, 1)
    )[0:8]
    sum_q = contract(dq_b, feat[...], 1, 0)
    sum_kv = (
        contract(kv_grad[...].astype(BF16), ext[...], 1, 0)
        + contract(slot_grad, slotf[...], 1, 0)
        + contract(virt_hi[:, 0:VROWS], virt[...], 1, 0)
        + contract(virt_lo[:, 0:VROWS], virt[...], 1, 0)
    )
    sum_o = contract(out_b, out_grad[...], 1, 0)
    for chunk in range(width // LANES):
        cols = slice(chunk * LANES, (chunk + 1) * LANES)
        weight_sums[chunk, 0:width] = sum_q[:, cols].astype(BF16)
        weight_sums[chunk, width : 3 * width] = sum_kv[:, cols].astype(BF16)
        weight_sums[chunk, 3 * width :] = sum_o[:, cols].astype(BF16)


def gather_kernel(
    sizes,
    slot_feat,
    halo_feat,
    sums,
    virt_feat,
    slots_back,
    halo_back,
    total,
    virt_total,
    got_c,
    sum_c,
    got_y,
    sum_y,
    got_x,
    sum_x,
    got_z,
    all_x,
    all_y,
    virt_c,
    virt_y,
    virt_x,
    virt_z,
    sems_a,
    sems_h,
    sems_c,
    sems_y,
    sems_x,
    sems_z,
    sems_gx,
    sems_gy,
    sems_gc,
    sems_v,
):
    nx, nz, ny = sizes
    n_dom, n_rows = nx * nz, 2 * ny
    dom, row = lax.axis_index("dom"), lax.axis_index("rows")
    x, z = dom // nz, lax.rem(dom, nz)
    y, core = row // 2, lax.rem(row, 2)
    mate = row + 1 - 2 * core
    chunks, height = sums.shape[0], sums.shape[1]
    half, quarter, piece = height // 2, height // 2 // ny, height // 2 // ny // nx

    def block(index, size):
        return pl.ds(pl.multiple_of(index * size, 16), size)

    barrier, arrivals = greet(n_dom, n_rows)
    virt_c[core] = virt_feat[...]
    pl.semaphore_wait(barrier, arrivals)

    def y_peer(step):
        return lax.rem(y + step, ny)

    def x_peer(step):
        return lax.rem(x + step, nx)

    def z_peer(step):
        return lax.rem(z + step, nz)

    def started(copies):
        for copy in copies:
            copy.start()
        return copies

    def waited(copies):
        for copy in copies:
            copy.wait()

    def to_core(ch):
        return [
            remote(
                sums.at[ch, block(1 - core, half)],
                got_c.at[ch],
                sems_c.at[0, ch],
                sems_c.at[1, ch],
                dom,
                mate,
            )
        ]

    def to_y(ch):
        return [
            remote(
                sum_c.at[ch, block(y_peer(s), quarter)],
                got_y.at[ch, s - 1],
                sems_y.at[0, ch, s],
                sems_y.at[1, ch, s],
                dom,
                y_peer(s) * 2 + core,
            )
            for s in range(1, ny)
        ]

    def to_x(ch):
        return [
            remote(
                sum_y.at[ch, block(x_peer(s), piece)],
                got_x.at[ch, s - 1],
                sems_x.at[0, ch, s],
                sems_x.at[1, ch, s],
                x_peer(s) * nz + z,
                row,
            )
            for s in range(1, nx)
        ]

    def to_z(ch):
        return [
            remote(
                sum_x.at[ch],
                got_z.at[ch, z],
                sems_z.at[0, ch, s],
                sems_z.at[1, ch, s],
                x * nz + z_peer(s),
                row,
            )
            for s in range(1, nz)
        ]

    def all_to_x(ch):
        return [
            remote(
                all_x.at[ch, block(x, piece)],
                all_x.at[ch, block(x, piece)],
                sems_gx.at[0, ch, s],
                sems_gx.at[1, ch, s],
                x_peer(s) * nz + z,
                row,
            )
            for s in range(1, nx)
        ]

    def all_to_y(ch):
        return [
            remote(
                all_x.at[ch],
                all_y.at[ch, block(y, quarter)],
                sems_gy.at[0, ch, s],
                sems_gy.at[1, ch, s],
                dom,
                y_peer(s) * 2 + core,
            )
            for s in range(1, ny)
        ]

    def all_to_core(ch):
        return [
            remote(
                all_y.at[ch],
                total.at[ch, block(core, half)],
                sems_gc.at[0, ch],
                sems_gc.at[1, ch],
                dom,
                mate,
            )
        ]

    def slot_copy(step):
        peer = lax.rem(dom + step, n_dom)
        return remote(
            slot_feat.at[peer],
            slots_back.at[dom],
            sems_a.at[0, step],
            sems_a.at[1, step],
            peer,
            row,
        )

    def slot_start(step, carry):
        slot_copy(step).start()
        return carry

    def slot_wait(step, carry):
        slot_copy(step).wait()
        return carry

    every = range(chunks)
    core_copies = [started(to_core(ch)) for ch in every]
    virt_core = started(
        [remote(virt_feat, virt_c.at[core], sems_v.at[0, 0], sems_v.at[1, 0], dom, mate)]
    )
    halo_copy = remote(
        halo_feat, halo_back, sems_h.at[0], sems_h.at[1], dom, lax.rem(row + n_rows - 1, n_rows)
    )
    halo_copy.start()
    lax.fori_loop(1, n_dom, slot_start, 0)
    slots_back[dom] = slot_feat[dom]

    y_copies = []
    for ch in every:
        waited(core_copies[ch])
        sum_c[ch] = (
            sums[ch, block(core, half)].astype(F32) + got_c[ch].astype(F32)
        ).astype(BF16)
        y_copies.append(started(to_y(ch)))
    waited(virt_core)
    virt_y[y] = virt_c[0] + virt_c[1]
    virt_ys = started(
        [
            remote(
                virt_y.at[y],
                virt_y.at[y],
                sems_v.at[0, s],
                sems_v.at[1, s],
                dom,
                y_peer(s) * 2 + core,
            )
            for s in range(1, ny)
        ]
    )
    x_copies = []
    for ch in every:
        waited(y_copies[ch])
        acc = sum_c[ch, block(y, quarter)].astype(F32)
        for s in range(ny - 1):
            acc = acc + got_y[ch, s].astype(F32)
        sum_y[ch] = acc.astype(BF16)
        x_copies.append(started(to_x(ch)))
    waited(virt_ys)
    total_v = virt_y[0]
    for s in range(1, ny):
        total_v = total_v + virt_y[s]
    virt_x[x] = total_v
    virt_xs = started(
        [
            remote(
                virt_x.at[x],
                virt_x.at[x],
                sems_v.at[0, ny + s],
                sems_v.at[1, ny + s],
                x_peer(s) * nz + z,
                row,
            )
            for s in range(1, nx)
        ]
    )
    z_copies = []
    for ch in every:
        waited(x_copies[ch])
        acc = sum_y[ch, block(x, piece)].astype(F32)
        for s in range(nx - 1):
            acc = acc + got_x[ch, s].astype(F32)
        sum_x[ch] = acc.astype(BF16)
        z_copies.append(started(to_z(ch)))
        got_z[ch, z] = sum_x[ch]
    waited(virt_xs)
    total_v = virt_x[0]
    for s in range(1, nx):
        total_v = total_v + virt_x[s]
    virt_z[z] = total_v
    virt_zs = started(
        [
            remote(
                virt_z.at[z],
                virt_z.at[z],
                sems_v.at[0, ny + nx + s],
                sems_v.at[1, ny + nx + s],
                x * nz + z_peer(s),
                row,
            )
            for s in range(1, nz)
        ]
    )
    gx_copies = []
    for ch in every:
        waited(z_copies[ch])
        acc = got_z[ch, 0].astype(F32)
        for s in range(1, nz):
            acc = acc + got_z[ch, s].astype(F32)
        all_x[ch, block(x, piece)] = acc.astype(BF16)
        gx_copies.append(started(all_to_x(ch)))
    waited(virt_zs)
    total_v = virt_z[0]
    for s in range(1, nz):
        total_v = total_v + virt_z[s]
    virt_total[...] = total_v
    gy_copies = []
    for ch in every:
        waited(gx_copies[ch])
        gy_copies.append(started(all_to_y(ch)))
        all_y[ch, block(y, quarter)] = all_x[ch]
    gc_copies = []
    for ch in every:
        waited(gy_copies[ch])
        gc_copies.append(started(all_to_core(ch)))
        total[ch, block(core, half)] = all_y[ch]
    for ch in every:
        waited(gc_copies[ch])
    halo_copy.wait()
    lax.fori_loop(1, n_dom, slot_wait, 0)


def finish_kernel(
    factor, send_flat, slots_back, halo_back, total, virt_total, grad_feat, gf, gq, gkv, go, gv
):
    row_count, width = gf.shape
    picker = row_picker(send_flat[...], row_count)
    summed = grad_feat[...].T + contract(picker, slots_back[...], 1, 0)
    gf[0 : row_count - TILE] = summed[0 : row_count - TILE]
    gf[row_count - TILE :] = summed[row_count - TILE :] + halo_back[...].astype(F32)
    for chunk in range(width // LANES):
        cols = slice(chunk * LANES, (chunk + 1) * LANES)
        part = total[chunk].astype(F32) * factor
        gq[cols, :] = part[0:width].T
        gkv[cols, 0:width] = part[width : 2 * width].T
        gkv[cols, width:] = part[2 * width : 3 * width].T
        go[:, cols] = part[3 * width :]
    gv[...] = virt_total[0:4] * factor


def shards(sizes, features, out_grad, w_query, w_keyval, w_out, virtual, local_nbr, expander, send_rows):
    nx, nz, ny = sizes
    n_dom, n_rows = nx * nz, 2 * ny
    rows, width = features.shape
    per_peer = send_rows.shape[1]
    slots = n_dom * per_peer
    send_flat = send_rows.reshape(1, slots)
    dma, shape = pltpu.SemaphoreType.DMA, jax.ShapeDtypeStruct
    slotf, halo = pl.pallas_call(
        functools.partial(spread_kernel, n_dom, n_rows),
        name="spread",
        out_shape=(shape((n_dom, per_peer, width), BF16), shape((TILE, width), BF16)),
        in_specs=[VMEM] * 2,
        out_specs=(VMEM, VMEM),
        scratch_shapes=[
            pltpu.VMEM((n_dom, per_peer, width), BF16),
            dma((n_dom,)),
            dma((n_dom,)),
            dma(()),
            dma(()),
        ],
        compiler_params=pltpu.CompilerParams(collective_id=0, has_side_effects=True),
    )(send_flat, features)

    slot_feat, halo_feat, sums, virt_feat, grad_feat = pl.pallas_call(
        attend_kernel,
        name="attend",
        out_shape=(
            shape((slots, width), BF16),
            shape((TILE, width), BF16),
            shape((width // LANES, 4 * width, LANES), BF16),
            shape((8, width), F32),
            shape((width, rows), F32),
        ),
        in_specs=[VMEM] * 10,
        out_specs=(VMEM,) * 5,
        scratch_shapes=[
            pltpu.VMEM((rows + TILE, width), BF16),
            pltpu.VMEM((width, rows), BF16),
            pltpu.VMEM((width, rows), BF16),
            pltpu.VMEM((2 * width, rows + TILE), BF16),
            pltpu.VMEM((2 * width, slots), BF16),
            pltpu.VMEM((slots, 4 * rows), BF16),
            pltpu.VMEM((4, 2 * width, rows), BF16),
            pltpu.VMEM((2 * TILE, rows), F32),
            pltpu.VMEM((HEADS, 8, rows), F32),
            pltpu.VMEM((HEADS, 8, rows), F32),
            pltpu.VMEM((HEADS, 8, rows), F32),
            pltpu.VMEM((HEADS, 8, rows), F32),
            pltpu.VMEM((2 * width, rows + TILE), F32),
            pltpu.VMEM((width, rows), F32),
            pltpu.VMEM((width, rows), F32),
            pltpu.VMEM((2 * width, 4 * rows), BF16),
        ],
        compiler_params=pltpu.CompilerParams(vmem_limit_bytes=60 << 20),
    )(
        features,
        halo,
        slotf.reshape(slots, width),
        out_grad,
        w_query,
        w_keyval,
        w_out,
        jnp.pad(virtual, ((0, VROWS - virtual.shape[0]), (0, 0))),
        local_nbr.T,
        expander.T,
    )

    chunks, height = sums.shape[0], sums.shape[1]
    half = height // 2
    quarter = half // ny
    piece = quarter // nx
    slots_back, halo_back, total, virt_total = pl.pallas_call(
        functools.partial(gather_kernel, sizes),
        name="gather",
        out_shape=(
            shape((n_dom, per_peer, width), BF16),
            shape((TILE, width), BF16),
            shape(sums.shape, BF16),
            shape((8, width), F32),
        ),
        in_specs=[VMEM] * 4,
        out_specs=(VMEM,) * 4,
        scratch_shapes=[
            pltpu.VMEM((chunks, half, LANES), BF16),
            pltpu.VMEM((chunks, half, LANES), BF16),
            pltpu.VMEM((chunks, ny - 1, quarter, LANES), BF16),
            pltpu.VMEM((chunks, quarter, LANES), BF16),
            pltpu.VMEM((chunks, nx - 1, piece, LANES), BF16),
            pltpu.VMEM((chunks, piece, LANES), BF16),
            pltpu.VMEM((chunks, nz, piece, LANES), BF16),
            pltpu.VMEM((chunks, quarter, LANES), BF16),
            pltpu.VMEM((chunks, half, LANES), BF16),
            pltpu.VMEM((2, 8, width), F32),
            pltpu.VMEM((ny, 8, width), F32),
            pltpu.VMEM((nx, 8, width), F32),
            pltpu.VMEM((nz, 8, width), F32),
            dma((2, n_dom)),
            dma((2,)),
            dma((2, chunks)),
            dma((2, chunks, ny)),
            dma((2, chunks, nx)),
            dma((2, chunks, nz)),
            dma((2, chunks, nx)),
            dma((2, chunks, ny)),
            dma((2, chunks)),
            dma((2, nx + ny + nz)),
        ],
        compiler_params=pltpu.CompilerParams(collective_id=1, has_side_effects=True),
    )(slot_feat.reshape(n_dom, per_peer, width), halo_feat, sums, virt_feat)

    return pl.pallas_call(
        functools.partial(finish_kernel, (rows * n_dom * n_rows) ** (-0.5)),
        name="finish",
        out_shape=(
            shape((rows, width), F32),
            shape((width, width), F32),
            shape((width, 2 * width), F32),
            shape((width, width), F32),
            shape((virtual.shape[0], width), F32),
        ),
        in_specs=[VMEM] * 6,
        out_specs=(VMEM,) * 5,
    )(send_flat, slots_back.reshape(slots, width), halo_back, total, virt_total, grad_feat)


def solution(mesh):
    n_dom, n_rows = mesh.shape["dom"], mesh.shape["rows"]
    nx = 4 if n_dom % 32 == 0 else 2
    sizes = (nx, n_dom // nx, n_rows // 2)
    across = P(("dom", "rows"), None)
    placed = (across, across, P(), P(), P(), P(), across, across, across)
    return jax.shard_map(
        functools.partial(shards, sizes),
        mesh=mesh,
        in_specs=placed,
        out_specs=(across, P(), P(), P(), P()),
        check_vma=False,
    )
```

time: 456 us -> 104 us (0.23)
  waiting for transfers between devices: 212 us -> 0 us
  Pallas kernels: 0 us -> 100 us
  blocking collectives: 78.5 us -> 0 us
  local copies, waits for them, and re-layouts: 58.6 us -> 2.67 us
  other arithmetic: 39.9 us -> 0 us
  matrix products: 27.4 us -> 0 us
  starting transfers between devices: 23.4 us -> 0 us
  between operations: 14.8 us -> 0.65 us
    psum x1 -> x0, waiting for transfers between devices: 173 us -> none  [shards(): lax.psum((rows_contracted(features, grad_query), rows_contracted(features...]
    pallas_call x0 -> x4, Pallas kernels: none -> 100 us  [the longest x1 48.9 us: shards(): pl.pallas_call(functools.partial(gather_kernel, sizes), name='gather', ou...]
    psum x1 -> x0, blocking collectives: 78.5 us -> none  [shards(): lax.psum((rows_contracted(features, grad_query), rows_contracted(features...]
    all_to_all x2 -> x0, waiting for transfers between devices: 37.2 us -> none  [the longest x1 28.7 us: shards(): lax.all_to_all(slot_grad, 'dom', split_axis=0, concat_axis=0, tiled=True)]
    dot_general x25 -> x0, matrix products: 27.4 us -> none  [the longest x12 12.9 us: einsum_bf(): return jnp.einsum(spec, left, right, preferred_element_type=jnp.float32)]
    all_to_all x2 -> x0, starting transfers between devices: 19.8 us -> none  [the longest x1 12 us: shards(): lax.all_to_all(key_value[send_flat], 'dom', split_axis=0, concat_axis=0,...]
    gather x4 -> x0, local copies, waits for them, and re-layouts: 18.3 us -> none  [the longest x2 8.1 us: shards(): expand_kv = slot_kv[expander]]
    scatter-add x2 -> x0, other arithmetic: 16.9 us -> none  [the longest x1 9.95 us: shards(): jax.ops.segment_sum(exp_grad.reshape(-1, 2 * feat_width), expander.reshap...]
  transfers between devices with their start and end apart: 5 -> 0, of which waited for: 4 -> 0; matrix products, arithmetic and copies ran while one was open for 9% -> 0% of each run, Pallas kernels for 0% -> 0%
where the time goes in v1:
time: 104 us
  Pallas kernels  100 us (96%)
  local copies, waits for them, and re-layouts  2.67 us (3%)
    pallas_call x1, Pallas kernels, shards(): pl.pallas_call(functools.partial(gather_kernel, sizes), name='gather', ou...  48.9 us
    pallas_call x1, Pallas kernels, shards(): pl.pallas_call(functools.partial(spread_kernel, n_dom, n_rows), name='spr...  30.4 us
    pallas_call x1, Pallas kernels, shards(): pl.pallas_call(attend_kernel, name='attend', out_shape=(shape((slots, wid...  17.4 us
    pallas_call x1, Pallas kernels, shards(): pl.pallas_call(functools.partial(finish_kernel, (rows * n_dom * n_rows) *...  3.74 us

profile of v1, /device:TPU:1, one launch (start us, length us, event | category | flops | bytes accessed | tf_op | source)
XLA Modules:
  0.0 103.8 jit_solution(2784605556108977378)
XLA Ops:
  0.6 1.4 %reshape.22.send_flat = s32[1,1024]{1,0:T(1,128)} reshape(s32[32,32]{1,0:T(8,128)} %param.17) | data formatting | bytes 8192 | tf_op jit(solution)/shard_map/reshape | solution.py:594
  2.0 1.3 %pad.4.virt = bf16[16,384]{1,0:T(8,128)(2,1)} pad(bf16[4,384]{1,0:T(4,128)(2,1)} %param.14, bf16[]{:T(256)} %constant.2.clone.1), padding=0_12x0_0 | pad | bytes 15362 | tf_op jit(solution)/shard_map/jit(_pad)/pad | solution.py:651
  3.3 30.4 %spread.1 = (bf16[32,32,384]{2,1,0:T(8,128)(2,1)}, bf16[128,384]{1,0:T(8,128)(2,1)}) custom-call(s32[1,1024]{1,0:T(1,128)} %reshape.22.send_flat, bf16[256,384]{1,0:T(8,128)(2,1)} %feat.3), custom_call_target="tpu_custom_call" | custom-call | tf_op jit(solution)/shard_map/spread/pallas_call | solution.py:596
  33.7 17.4 %attend.1 = (bf16[1024,384]{1,0:T(8,128)(2,1)}, bf16[128,384]{1,0:T(8,128)(2,1)}, bf16[3,1536,128]{2,1,0:T(8,128)(2,1)}, f32[8,384]{1,0:T(8,128)}, f32[384,256]{1,0:T(8,128)}) custom-call(bf16[256,384]{1,0:T(8,128)(2,1)} %feat.3, bf16[128,384]{1,0:T(8,128)(2,1)} %get-tuple-element.16.halo, bf16[1024,384]{1,0:T(8,128)(2,1)} %bitcast.5, ...), custom_call_target="tpu_custom_call" | custom-call | tf_op jit(solution)/shard_map/attend/pallas_call | solution.py:612
  51.1 48.9 %gather.1 = (bf16[32,32,384]{2,1,0:T(8,128)(2,1)}, bf16[128,384]{1,0:T(8,128)(2,1)}, bf16[3,1536,128]{2,1,0:T(8,128)(2,1)}, f32[8,384]{1,0:T(8,128)}) custom-call(bf16[32,32,384]{2,1,0:T(8,128)(2,1)} %bitcast.7, bf16[128,384]{1,0:T(8,128)(2,1)} %get-tuple-element.19.halo_feat, bf16[3,1536,128]{2,1,0:T(8,128)(2,1)} %get-tuple-element.20.sums, ...), custom_call_target="tpu_custom_call" | custom-call | tf_op jit(solution)/shard_map/gather/pallas_call | solution.py:660
  100.0 3.7 %finish.1 = (f32[256,384]{1,0:T(8,128)}, f32[384,384]{1,0:T(8,128)}, f32[384,768]{1,0:T(8,128)}, f32[384,384]{1,0:T(8,128)}, f32[4,384]{1,0:T(4,128)}) custom-call(s32[1,1024]{1,0:T(1,128)} %reshape.22.send_flat, bf16[1024,384]{1,0:T(8,128)(2,1)} %bitcast.6, bf16[128,384]{1,0:T(8,128)(2,1)} %get-tuple-element.23.halo_back, ...), custom_call_target="tpu_custom_call" | custom-call | tf_op jit(solution)/shard_map/finish/pallas_call | solution.py:699

commit v2 on v0

v2 whole, which is shorter than its diff:
```python
import functools
import math

import jax
import jax.numpy as jnp
from jax import lax
from jax.experimental import pallas as pl
from jax.experimental.pallas import tpu as pltpu
from jax.sharding import PartitionSpec as P

HEADS = 8
TILE = 128
LANES = 128
VROWS = 16
NEGATIVE_FILL = -1e30

F32 = jnp.float32
BF16 = jnp.bfloat16
VMEM = pl.BlockSpec(memory_space=pltpu.VMEM)


def contract(left, right, left_dim, right_dim):
    return lax.dot_general(
        left, right, (((left_dim,), (right_dim,)), ((), ())), preferred_element_type=F32
    )


def remote(src, dst, send_sem, recv_sem, dom, row):
    return pltpu.make_async_remote_copy(
        src_ref=src,
        dst_ref=dst,
        send_sem=send_sem,
        recv_sem=recv_sem,
        device_id=(dom, row),
        device_id_type=pl.DeviceIdType.MESH,
    )


def greet(n_dom, n_rows):
    dom, row = lax.axis_index("dom"), lax.axis_index("rows")
    barrier = pltpu.get_barrier_semaphore()

    def dom_peer(step, carry):
        pl.semaphore_signal(
            barrier,
            inc=1,
            device_id=(lax.rem(dom + step, n_dom), row),
            device_id_type=pl.DeviceIdType.MESH,
        )
        return carry

    def row_peer(step, carry):
        pl.semaphore_signal(
            barrier,
            inc=1,
            device_id=(dom, lax.rem(row + step, n_rows)),
            device_id_type=pl.DeviceIdType.MESH,
        )
        return carry

    lax.fori_loop(1, n_dom, dom_peer, 0)
    lax.fori_loop(1, n_rows, row_peer, 0)
    return barrier, n_dom + n_rows - 2


def whole_kernel(
    sizes,
    feat,
    out_grad,
    w_query,
    w_keyval,
    w_out,
    virt,
    local_nbr,
    expander,
    send_rows,
    grad_feat,
    total,
    virt_total,
    picker,
    picked,
    slots,
    halo,
    virt_pad,
    wkv_t,
    ext_t,
    slot_t,
    q_t,
    d_t,
    kv_t,
    named,
    bias,
    edge_kv,
    weight_e,
    weight_dp,
    rows_s,
    rows_f,
    rows_d,
    kv_grad,
    out_t,
    dq_t,
    edge_grad,
    slot_grad,
    slot_feat,
    halo_feat,
    slots_back,
    halo_back,
    sums,
    got_c,
    sum_c,
    got_y,
    sum_y,
    got_x,
    sum_x,
    got_z,
    all_x,
    all_y,
    virt_feat,
    virt_c,
    virt_y,
    virt_x,
    virt_z,
    sems_s,
    sems_g,
    sems_a,
    sems_h,
    sems_c,
    sems_y,
    sems_x,
    sems_z,
    sems_gx,
    sems_gy,
    sems_gc,
    sems_v,
):
    nx, nz, ny = sizes
    n_dom, n_rows = nx * nz, 2 * ny
    dom, row = lax.axis_index("dom"), lax.axis_index("rows")
    x, z = dom // nz, lax.rem(dom, nz)
    y, core = row // 2, lax.rem(row, 2)
    mate = row + 1 - 2 * core
    row_count, width = feat.shape
    per_peer = send_rows.shape[1]
    slot_count = n_dom * per_peer
    head_dim = width // HEADS
    degree = expander.shape[0]
    scale = 1.0 / math.sqrt(head_dim)
    tiles = row_count // TILE
    bits = per_peer.bit_length() - 1
    groups = 4
    per_group = n_dom // groups
    span = per_group * per_peer

    barrier, arrivals = greet(n_dom, n_rows)

    spot = lax.broadcasted_iota(jnp.int32, (per_peer, slot_count), 1)
    entry = lax.broadcasted_iota(jnp.int32, (per_peer, slot_count), 0)
    spread = (jnp.bitwise_and(spot, per_peer - 1) == entry).astype(F32).astype(BF16)
    listed = contract(send_rows[...].astype(F32).astype(BF16), spread, 1, 0)
    owner = lax.broadcasted_iota(jnp.int32, (n_dom, slot_count), 0)
    column = lax.broadcasted_iota(jnp.int32, (n_dom, slot_count), 1)
    mine = jnp.right_shift(column, bits) == owner
    send_flat = jnp.sum(jnp.where(mine, listed, 0.0), axis=0, keepdims=True).astype(jnp.int32)
    rows_at = lax.broadcasted_iota(jnp.int32, (row_count, slot_count), 0)
    picker[...] = (rows_at == send_flat).astype(F32).astype(BF16)
    picked[...] = contract(picker[...], feat[...], 0, 0).astype(BF16).reshape(picked.shape)

    pl.semaphore_wait(barrier, arrivals)

    halo_copy = remote(
        feat.at[pl.ds(row_count - TILE, TILE)],
        halo,
        sems_h.at[0],
        sems_h.at[1],
        dom,
        lax.rem(row + 1, n_rows),
    )
    halo_copy.start()

    def spread_copy(step):
        peer = lax.rem(dom + step, n_dom)
        return remote(
            picked.at[peer], slots.at[step], sems_s.at[0, step], sems_s.at[1, step], peer, row
        )

    def spread_start(step, carry):
        spread_copy(step).start()
        return carry

    def spread_wait(step, carry):
        spread_copy(step).wait()
        return carry

    lax.fori_loop(1, n_dom, spread_start, 0)
    slots[0] = picked[dom]

    wkv_t[...] = w_keyval[...].T
    ext_t[:, TILE:] = feat[...].T
    q_t[...] = contract(w_query[...], ext_t[:, TILE:], 0, 0).astype(BF16)
    d_t[...] = contract(w_out[...], out_grad[...], 1, 1).astype(BF16)
    kv_t[:, TILE:] = contract(wkv_t[...], ext_t[:, TILE:], 1, 0).astype(BF16)
    virt_pad[...] = jnp.zeros_like(virt_pad)
    virt_pad[0 : virt.shape[0]] = virt[...].astype(F32)
    virt_b = virt_pad[...].astype(BF16)
    virt_kv = contract(wkv_t[...], virt_b, 1, 1).astype(BF16).astype(F32)

    positions = lax.broadcasted_iota(jnp.int32, (2 * TILE, row_count), 0)
    mask = positions == local_nbr[0:1, :]
    for place in range(1, local_nbr.shape[0]):
        mask = jnp.logical_or(mask, positions == local_nbr[place : place + 1, :])
    bias[...] = jnp.where(mask, 0.0, NEGATIVE_FILL)

    source = jnp.right_shift(expander[...], bits)
    away = dom - source
    away = jnp.where(away < 0, away + n_dom, away)
    slot_of = away * per_peer + jnp.bitwise_and(expander[...], per_peer - 1)
    slot_ids = lax.broadcasted_iota(jnp.int32, (slot_count, row_count), 0)
    for k in range(degree):
        named[:, k * row_count : (k + 1) * row_count] = (
            (slot_ids == slot_of[k : k + 1, :]).astype(F32).astype(BF16)
        )

    def per_head(product):
        return product.reshape(HEADS, head_dim, row_count).sum(axis=1)

    def virtual_edge(v):
        return jnp.broadcast_to(virt_kv[:, v : v + 1], (2 * width, row_count))

    virt_s, virt_dp = [], []
    for v in range(4):
        both = virtual_edge(v)
        virt_s.append(per_head(q_t[...].astype(F32) * both[0:width]) * scale)
        virt_dp.append(per_head(d_t[...].astype(F32) * both[width:]))

    halo_copy.wait()
    ext_t[:, 0:TILE] = halo[...].T
    kv_t[:, 0:TILE] = contract(wkv_t[...], ext_t[:, 0:TILE], 1, 0).astype(BF16)

    def places(h, t):
        own = slice(h * head_dim, (h + 1) * head_dim)
        val = slice(width + h * head_dim, width + (h + 1) * head_dim)
        return own, val, slice(t * TILE, (t + 1) * TILE), slice(t * TILE, (t + 2) * TILE)

    for h in range(HEADS):
        for t in range(tiles):
            own, val, here, window = places(h, t)
            s = contract(kv_t[own, window], q_t[own, here], 0, 0) * scale + bias[:, here]
            dp = contract(kv_t[val, window], d_t[own, here], 0, 0)
            peak = jnp.max(s, axis=0, keepdims=True)
            e = jnp.exp(s - peak)
            weight_e[h, t] = e
            weight_dp[h, t] = dp
            rows_s[h : h + 1, here] = peak
            rows_f[h : h + 1, here] = jnp.sum(e, axis=0, keepdims=True)
            rows_d[h : h + 1, here] = jnp.sum(e * dp, axis=0, keepdims=True)

    for g in range(groups):
        lax.fori_loop(max(1, g * per_group), (g + 1) * per_group, spread_wait, 0)
        held = slice(g * span, (g + 1) * span)
        slot_t[:, held] = slots[g * per_group : (g + 1) * per_group].reshape(span, width).T
        slot_kv = contract(wkv_t[...], slot_t[:, held], 1, 0).astype(BF16)
        chosen = contract(slot_kv, named[held, :], 1, 0)
        if g == 0:
            edge_kv[...] = chosen
        else:
            edge_kv[...] += chosen

    q_wide = q_t[...].astype(F32)
    d_wide = d_t[...].astype(F32)
    cols = [slice(k * row_count, (k + 1) * row_count) for k in range(degree)]
    edge_s = [per_head(q_wide * edge_kv[0:width, c]) * scale for c in cols] + virt_s
    edge_dp = [per_head(d_wide * edge_kv[width:, c]) for c in cols] + virt_dp
    peak_loc = rows_s[...]
    peak = peak_loc
    for s in edge_s:
        peak = jnp.maximum(peak, s)
    shrink = jnp.exp(peak_loc - peak)
    edge_e = [jnp.exp(s - peak) for s in edge_s]
    norm = rows_f[...] * shrink
    for e in edge_e:
        norm = norm + e
    inverse = 1.0 / norm
    edge_p = [e * inverse for e in edge_e]
    share = shrink * inverse
    delta = rows_d[...] * share
    for p, dp in zip(edge_p, edge_dp):
        delta = delta + p * dp
    rows_f[...] = share
    rows_d[...] = delta
    edge_ds = [
        (p * (dp - delta) * scale).astype(BF16).astype(F32) for p, dp in zip(edge_p, edge_dp)
    ]
    edge_p = [p.astype(BF16).astype(F32) for p in edge_p]

    def widen(values):
        return jnp.broadcast_to(values[:, None, :], (HEADS, head_dim, row_count)).reshape(
            width, row_count
        )

    out_sum = jnp.zeros((width, row_count), F32)
    dq_sum = jnp.zeros((width, row_count), F32)
    for k in range(degree):
        pk, dsk = widen(edge_p[k]), widen(edge_ds[k])
        out_sum = out_sum + pk * edge_kv[width:, cols[k]]
        dq_sum = dq_sum + dsk * edge_kv[0:width, cols[k]]
        edge_grad[0:width, cols[k]] = (dsk * q_wide).astype(BF16)
        edge_grad[width:, cols[k]] = (pk * d_wide).astype(BF16)
    out_t[...] = out_sum
    dq_t[...] = dq_sum

    def back_copy(step):
        peer = lax.rem(dom - step + n_dom, n_dom)
        return remote(
            slot_feat.at[step],
            slots_back.at[dom],
            sems_g.at[0, step],
            sems_g.at[1, step],
            peer,
            row,
        )

    def back_start(step, carry):
        back_copy(step).start()
        return carry

    def back_wait(step, carry):
        back_copy(step).wait()
        return carry

    for g in range(groups):
        held = slice(g * span, (g + 1) * span)
        grad_g = contract(edge_grad[...], named[held, :], 1, 1).astype(BF16)
        slot_grad[:, held] = grad_g
        slot_feat[g * per_group : (g + 1) * per_group] = (
            contract(grad_g, w_keyval[...], 0, 1).astype(BF16).reshape(per_group, per_peer, width)
        )
        lax.fori_loop(max(1, g * per_group), (g + 1) * per_group, back_start, 0)
    slots_back[dom] = slot_feat[0]

    kv_grad[...] = jnp.zeros_like(kv_grad)
    for h in range(HEADS):
        for t in range(tiles):
            own, val, here, window = places(h, t)
            p = weight_e[h, t] * rows_f[h : h + 1, here]
            ds = (p * (weight_dp[h, t] - rows_d[h : h + 1, here]) * scale).astype(BF16)
            pb = p.astype(BF16)
            out_t[own, here] += contract(kv_t[val, window], pb, 1, 0)
            dq_t[own, here] += contract(kv_t[own, window], ds, 1, 0)
            kv_grad[own, window] += contract(q_t[own, here], ds, 1, 1)
            kv_grad[val, window] += contract(d_t[own, here], pb, 1, 1)

    lane = lax.broadcasted_iota(jnp.int32, (2 * width, LANES), 1)
    virt_t = jnp.zeros((2 * width, LANES), F32)
    out_sum = out_t[...]
    dq_sum = dq_t[...]
    for v in range(4):
        pk, dsk = widen(edge_p[degree + v]), widen(edge_ds[degree + v])
        both = virtual_edge(v)
        out_sum = out_sum + pk * both[width:]
        dq_sum = dq_sum + dsk * both[0:width]
        to_both = jnp.concatenate(
            [
                jnp.sum(dsk * q_wide, axis=1, keepdims=True),
                jnp.sum(pk * d_wide, axis=1, keepdims=True),
            ],
            axis=0,
        )
        virt_t = jnp.where(lane == v, to_both, virt_t)
    out_b = out_sum.astype(BF16)
    dq_b = dq_sum.astype(BF16)

    chunks, height = sums.shape[0], sums.shape[1]
    half, quarter, piece = height // 2, height // 2 // ny, height // 2 // ny // nx

    def put(block_index, value):
        first = block_index * width
        while value.shape[0]:
            ch, at = divmod(first, height)
            count = min(height - at, value.shape[0])
            sums[ch, at : at + count] = value[0:count]
            value = value[count:]
            first += count

    def block(index, size):
        return pl.ds(pl.multiple_of(index * size, 16), size)

    def y_peer(step):
        return lax.rem(y + step, ny)

    def x_peer(step):
        return lax.rem(x + step, nx)

    def z_peer(step):
        return lax.rem(z + step, nz)

    started = {}

    def start(key, copies):
        for copy in copies:
            copy.start()
        started[key] = copies

    def finish(key):
        for copy in started.pop(key):
            copy.wait()

    def stage_c(ch):
        start(
            ("c", ch),
            [
                remote(
                    sums.at[ch, block(1 - core, half)],
                    got_c.at[ch],
                    sems_c.at[0, ch],
                    sems_c.at[1, ch],
                    dom,
                    mate,
                )
            ],
        )

    def stage_y(ch):
        finish(("c", ch))
        sum_c[ch] = (sums[ch, block(core, half)].astype(F32) + got_c[ch].astype(F32)).astype(BF16)
        start(
            ("y", ch),
            [
                remote(
                    sum_c.at[ch, block(y_peer(s), quarter)],
                    got_y.at[ch, s - 1],
                    sems_y.at[0, ch, s],
                    sems_y.at[1, ch, s],
                    dom,
                    y_peer(s) * 2 + core,
                )
                for s in range(1, ny)
            ],
        )

    def stage_x(ch):
        finish(("y", ch))
        acc = sum_c[ch, block(y, quarter)].astype(F32)
        for s in range(ny - 1):
            acc = acc + got_y[ch, s].astype(F32)
        sum_y[ch] = acc.astype(BF16)
        start(
            ("x", ch),
            [
                remote(
                    sum_y.at[ch, block(x_peer(s), piece)],
                    got_x.at[ch, s - 1],
                    sems_x.at[0, ch, s],
                    sems_x.at[1, ch, s],
                    x_peer(s) * nz + z,
                    row,
                )
                for s in range(1, nx)
            ],
        )

    def stage_z(ch):
        finish(("x", ch))
        acc = sum_y[ch, block(x, piece)].astype(F32)
        for s in range(nx - 1):
            acc = acc + got_x[ch, s].astype(F32)
        sum_x[ch] = acc.astype(BF16)
        start(
            ("z", ch),
            [
                remote(
                    sum_x.at[ch],
                    got_z.at[ch, z],
                    sems_z.at[0, ch, s],
                    sems_z.at[1, ch, s],
                    x * nz + z_peer(s),
                    row,
                )
                for s in range(1, nz)
            ],
        )
        got_z[ch, z] = acc.astype(BF16)

    def stage_all_x(ch):
        finish(("z", ch))
        acc = got_z[ch, 0].astype(F32)
        for s in range(1, nz):
            acc = acc + got_z[ch, s].astype(F32)
        all_x[ch, block(x, piece)] = acc.astype(BF16)
        start(
            ("gx", ch),
            [
                remote(
                    all_x.at[ch, block(x, piece)],
                    all_x.at[ch, block(x, piece)],
                    sems_gx.at[0, ch, s],
                    sems_gx.at[1, ch, s],
                    x_peer(s) * nz + z,
                    row,
                )
                for s in range(1, nx)
            ],
        )

    def stage_all_y(ch):
        finish(("gx", ch))
        start(
            ("gy", ch),
            [
                remote(
                    all_x.at[ch],
                    all_y.at[ch, block(y, quarter)],
                    sems_gy.at[0, ch, s],
                    sems_gy.at[1, ch, s],
                    dom,
                    y_peer(s) * 2 + core,
                )
                for s in range(1, ny)
            ],
        )
        all_y[ch, block(y, quarter)] = all_x[ch]

    def stage_all_c(ch):
        finish(("gy", ch))
        start(
            ("gc", ch),
            [
                remote(
                    all_y.at[ch],
                    total.at[ch, block(core, half)],
                    sems_gc.at[0, ch],
                    sems_gc.at[1, ch],
                    dom,
                    mate,
                )
            ],
        )
        total[ch, block(core, half)] = all_y[ch]

    def virt_exchange(key, buffer, index, first, peers):
        start(
            key,
            [
                remote(
                    buffer.at[index],
                    buffer.at[index],
                    sems_v.at[0, first + s],
                    sems_v.at[1, first + s],
                    to_dom,
                    to_row,
                )
                for s, (to_dom, to_row) in enumerate(peers)
            ],
        )

    def virt_sum(key, buffer):
        finish(key)
        acc = buffer[0]
        for s in range(1, buffer.shape[0]):
            acc = acc + buffer[s]
        return acc

    def virt_stage(stage):
        if stage == 0:
            virt_c[core] = virt_feat[...]
            virt_exchange("vc", virt_c, core, 0, [(dom, mate)])
        elif stage == 1:
            virt_y[y] = virt_sum("vc", virt_c)
            virt_exchange(
                "vy", virt_y, y, 1, [(dom, y_peer(s) * 2 + core) for s in range(1, ny)]
            )
        elif stage == 2:
            virt_x[x] = virt_sum("vy", virt_y)
            virt_exchange(
                "vx", virt_x, x, ny, [(x_peer(s) * nz + z, row) for s in range(1, nx)]
            )
        elif stage == 3:
            virt_z[z] = virt_sum("vx", virt_x)
            virt_exchange(
                "vz", virt_z, z, ny + nx - 1, [(x * nz + z_peer(s), row) for s in range(1, nz)]
            )
        elif stage == 4:
            virt_total[...] = virt_sum("vz", virt_z)

    stages = [stage_c, stage_y, stage_x, stage_z, stage_all_x, stage_all_y, stage_all_c]

    put(0, contract(out_b, out_grad[...], 1, 0).astype(BF16))
    put(1, contract(ext_t[:, TILE:], dq_b, 1, 1).astype(BF16))
    stage_c(0)
    virt_hi = virt_t.astype(BF16)
    virt_lo = (virt_t - virt_hi.astype(F32)).astype(BF16)
    kv_sum = (
        contract(ext_t[...], kv_grad[...].astype(BF16), 1, 1)
        + contract(slot_t[...], slot_grad[...], 1, 1)
        + contract(virt_b, virt_hi[:, 0:VROWS], 0, 1)
        + contract(virt_b, virt_lo[:, 0:VROWS], 0, 1)
    ).astype(BF16)
    put(2, kv_sum[:, 0:width])
    put(3, kv_sum[:, width:])
    stage_c(1)
    stage_c(2)
    virt_feat[...] = (
        contract(virt_hi, w_keyval[...], 0, 1) + contract(virt_lo, w_keyval[...], 0, 1)
    )[0:8]
    virt_stage(0)
    halo_feat[...] = contract(kv_grad[:, 0:TILE].astype(BF16), w_keyval[...], 0, 1).astype(BF16)
    halo_return = remote(
        halo_feat,
        halo_back,
        sems_a.at[0],
        sems_a.at[1],
        dom,
        lax.rem(row + n_rows - 1, n_rows),
    )
    halo_return.start()
    stage_y(0)
    stage_y(1)
    stage_y(2)
    grad_t = contract(w_query[...], dq_b, 1, 0) + contract(
        w_keyval[...], kv_grad[:, TILE:].astype(BF16), 1, 0
    )
    grad_feat[...] = grad_t.T
    for diagonal in range(2, len(stages) + chunks):
        for ch in range(chunks):
            stage = diagonal - ch
            if 2 <= stage < len(stages):
                stages[stage](ch)
        virt_stage(diagonal - 1)
    halo_return.wait()
    lax.fori_loop(1, n_dom, back_wait, 0)
    summed = grad_feat[...] + contract(
        picker[...], slots_back[...].reshape(slot_count, width), 1, 0
    )
    grad_feat[0 : row_count - TILE] = summed[0 : row_count - TILE]
    grad_feat[row_count - TILE :] = summed[row_count - TILE :] + halo_back[...].astype(F32)
    for ch in range(chunks):
        finish(("gc", ch))


def finish_kernel(factor, go_in, gq_in, gk_in, gv_in, virt_in, feat_in, gq, gkv, go, gv, gf):
    width = gq.shape[1]
    gq[...] = gq_in[...].astype(F32) * factor
    go[...] = go_in[...].astype(F32) * factor
    gkv[:, 0:width] = gk_in[...].astype(F32) * factor
    gkv[:, width:] = gv_in[...].astype(F32) * factor

    @pl.when(pl.program_id(0) == 0)
    def _():
        gv[...] = virt_in[0 : gv.shape[0]] * factor
        gf[...] = feat_in[...]


def shards(sizes, features, out_grad, w_query, w_keyval, w_out, virtual, local_nbr, expander, send_rows):
    nx, nz, ny = sizes
    n_dom, n_rows = nx * nz, 2 * ny
    rows, width = features.shape
    per_peer = send_rows.shape[1]
    slots = n_dom * per_peer
    dma, shape = pltpu.SemaphoreType.DMA, jax.ShapeDtypeStruct
    chunks = 3
    height = 4 * width // chunks
    half = height // 2
    quarter = half // ny
    piece = quarter // nx
    tiles = rows // TILE
    grad_feat, total, virt_total = pl.pallas_call(
        functools.partial(whole_kernel, sizes),
        name="whole",
        out_shape=(
            shape((rows, width), F32),
            shape((chunks, height, width), BF16),
            shape((8, width), F32),
        ),
        in_specs=[VMEM] * 9,
        out_specs=(VMEM,) * 3,
        scratch_shapes=[
            pltpu.VMEM((rows, slots), BF16),
            pltpu.VMEM((n_dom, per_peer, width), BF16),
            pltpu.VMEM((n_dom, per_peer, width), BF16),
            pltpu.VMEM((TILE, width), BF16),
            pltpu.VMEM((VROWS, width), F32),
            pltpu.VMEM((2 * width, width), BF16),
            pltpu.VMEM((width, rows + TILE), BF16),
            pltpu.VMEM((width, slots), BF16),
            pltpu.VMEM((width, rows), BF16),
            pltpu.VMEM((width, rows), BF16),
            pltpu.VMEM((2 * width, rows + TILE), BF16),
            pltpu.VMEM((slots, 4 * rows), BF16),
            pltpu.VMEM((2 * TILE, rows), F32),
            pltpu.VMEM((2 * width, 4 * rows), F32),
            pltpu.VMEM((HEADS, tiles, 2 * TILE, TILE), F32),
            pltpu.VMEM((HEADS, tiles, 2 * TILE, TILE), F32),
            pltpu.VMEM((HEADS, rows), F32),
            pltpu.VMEM((HEADS, rows), F32),
            pltpu.VMEM((HEADS, rows), F32),
            pltpu.VMEM((2 * width, rows + TILE), F32),
            pltpu.VMEM((width, rows), F32),
            pltpu.VMEM((width, rows), F32),
            pltpu.VMEM((2 * width, 4 * rows), BF16),
            pltpu.VMEM((2 * width, slots), BF16),
            pltpu.VMEM((n_dom, per_peer, width), BF16),
            pltpu.VMEM((TILE, width), BF16),
            pltpu.VMEM((n_dom, per_peer, width), BF16),
            pltpu.VMEM((TILE, width), BF16),
            pltpu.VMEM((chunks, height, width), BF16),
            pltpu.VMEM((chunks, half, width), BF16),
            pltpu.VMEM((chunks, half, width), BF16),
            pltpu.VMEM((chunks, ny - 1, quarter, width), BF16),
            pltpu.VMEM((chunks, quarter, width), BF16),
            pltpu.VMEM((chunks, nx - 1, piece, width), BF16),
            pltpu.VMEM((chunks, piece, width), BF16),
            pltpu.VMEM((chunks, nz, piece, width), BF16),
            pltpu.VMEM((chunks, quarter, width), BF16),
            pltpu.VMEM((chunks, half, width), BF16),
            pltpu.VMEM((8, width), F32),
            pltpu.VMEM((2, 8, width), F32),
            pltpu.VMEM((ny, 8, width), F32),
            pltpu.VMEM((nx, 8, width), F32),
            pltpu.VMEM((nz, 8, width), F32),
            dma((2, n_dom)),
            dma((2, n_dom)),
            dma((2,)),
            dma((2,)),
            dma((2, chunks)),
            dma((2, chunks, ny)),
            dma((2, chunks, nx)),
            dma((2, chunks, nz)),
            dma((2, chunks, nx)),
            dma((2, chunks, ny)),
            dma((2, chunks)),
            dma((2, nx + ny + nz)),
        ],
        compiler_params=pltpu.CompilerParams(
            collective_id=0, has_side_effects=True, vmem_limit_bytes=60 << 20
        ),
    )(
        features,
        out_grad,
        w_query,
        w_keyval,
        w_out,
        virtual,
        local_nbr.T,
        expander.T,
        send_rows,
    )

    flat = total.reshape(chunks * height, width)
    steps = width // LANES

    def rows_of(part):
        return pl.BlockSpec((LANES, width), lambda i: (part * steps + i, 0))

    def fixed(count):
        return pl.BlockSpec((count, width), lambda i: (0, 0))

    gq, gkv, go, gv, gf = pl.pallas_call(
        functools.partial(finish_kernel, (rows * n_dom * n_rows) ** (-0.5)),
        name="finish",
        grid=(steps,),
        out_shape=(
            shape((width, width), F32),
            shape((width, 2 * width), F32),
            shape((width, width), F32),
            shape((virtual.shape[0], width), F32),
            shape((rows, width), F32),
        ),
        in_specs=[rows_of(0), rows_of(1), rows_of(2), rows_of(3), fixed(8), fixed(rows)],
        out_specs=(
            rows_of(0),
            pl.BlockSpec((LANES, 2 * width), lambda i: (i, 0)),
            rows_of(0),
            fixed(virtual.shape[0]),
            fixed(rows),
        ),
    )(flat, flat, flat, flat, virt_total, grad_feat)
    return gf, gq, gkv, go, gv


def solution(mesh):
    n_dom, n_rows = mesh.shape["dom"], mesh.shape["rows"]
    nx = 4 if n_dom % 32 == 0 else 2
    sizes = (nx, n_dom // nx, n_rows // 2)
    across = P(("dom", "rows"), None)
    placed = (across, across, P(), P(), P(), P(), across, across, across)
    return jax.shard_map(
        functools.partial(shards, sizes),
        mesh=mesh,
        in_specs=placed,
        out_specs=(across, P(), P(), P(), P()),
        check_vma=False,
    )
```

time: 456 us -> 92 us (0.20)
  waiting for transfers between devices: 212 us -> 0 us
  Pallas kernels: 0 us -> 91 us
  blocking collectives: 78.5 us -> 0 us
  local copies, waits for them, and re-layouts: 58.6 us -> 0 us
  other arithmetic: 39.9 us -> 0 us
  matrix products: 27.4 us -> 0 us
  starting transfers between devices: 23.4 us -> 0 us
  between operations: 14.8 us -> 0.8 us
    psum x1 -> x0, waiting for transfers between devices: 173 us -> none  [shards(): lax.psum((rows_contracted(features, grad_query), rows_contracted(features...]
    pallas_call x0 -> x2, Pallas kernels: none -> 91 us  [the longest x1 87 us: shards(): pl.pallas_call(functools.partial(whole_kernel, sizes), name='whole', out_...]
    psum x1 -> x0, blocking collectives: 78.5 us -> none  [shards(): lax.psum((rows_contracted(features, grad_query), rows_contracted(features...]
    all_to_all x2 -> x0, waiting for transfers between devices: 37.2 us -> none  [the longest x1 28.7 us: shards(): lax.all_to_all(slot_grad, 'dom', split_axis=0, concat_axis=0, tiled=True)]
    dot_general x25 -> x0, matrix products: 27.4 us -> none  [the longest x12 12.9 us: einsum_bf(): return jnp.einsum(spec, left, right, preferred_element_type=jnp.float32)]
    all_to_all x2 -> x0, starting transfers between devices: 19.8 us -> none  [the longest x1 12 us: shards(): lax.all_to_all(key_value[send_flat], 'dom', split_axis=0, concat_axis=0,...]
    gather x4 -> x0, local copies, waits for them, and re-layouts: 18.3 us -> none  [the longest x2 8.1 us: shards(): expand_kv = slot_kv[expander]]
    scatter-add x2 -> x0, other arithmetic: 16.9 us -> none  [the longest x1 9.95 us: shards(): jax.ops.segment_sum(exp_grad.reshape(-1, 2 * feat_width), expander.reshap...]
  transfers between devices with their start and end apart: 5 -> 0, of which waited for: 4 -> 0; matrix products, arithmetic and copies ran while one was open for 9% -> 0% of each run, Pallas kernels for 0% -> 0%
where the time goes in v2:
time: 92 us; the launch traced here: 91.8 us
  Pallas kernels  91 us (99%)
    pallas_call x1, Pallas kernels, shards(): pl.pallas_call(functools.partial(whole_kernel, sizes), name='whole', out_...  87 us
    pallas_call x1, Pallas kernels, shards(): pl.pallas_call(functools.partial(finish_kernel, (rows * n_dom * n_rows) *...  3.97 us

profile of v2, /device:TPU:1, one launch (start us, length us, event | category | flops | bytes accessed | tf_op | source)
XLA Modules:
  0.0 91.8 jit_solution(1449371923873060169)
XLA Ops:
  0.6 87.0 %whole.1 = (f32[256,384]{1,0:T(8,128)}, bf16[3,512,384]{2,1,0:T(8,128)(2,1)}, f32[8,384]{1,0:T(8,128)}) custom-call(bf16[256,384]{1,0:T(8,128)(2,1)} %feat.1, bf16[256,384]{1,0:T(8,128)(2,1)} %out_grad.1, bf16[384,384]{1,0:T(8,128)(2,1)} %w_query.1, bf16[384,768]{1,0:T(8,128)(2,1)} %w_keyval.1, bf16[384,384]{1,0:T(8,128)(2,1)} %w_out.1, ...), custom_call_target="tpu_custom_call" | custom-call | tf_op jit(solution)/shard_map/whole/pallas_call | solution.py:665
  87.6 4.0 %finish.1 = (f32[384,384]{1,0:T(8,128)}, f32[384,768]{1,0:T(8,128)}, f32[384,384]{1,0:T(8,128)}, f32[4,384]{1,0:T(4,128)}, f32[256,384]{1,0:T(8,128)}) custom-call(bf16[1536,384]{1,0:T(8,128)(2,1)} %bitcast.3, bf16[1536,384]{1,0:T(8,128)(2,1)} %bitcast.4, bf16[1536,384]{1,0:T(8,128)(2,1)} %bitcast.5, bf16[1536,384]{1,0:T(8,128)(2,1)} %bitcast.6, ...), custom_call_target="tpu_custom_call" | custom-call | tf_op jit(solution)/shard_map/finish/pallas_call | solution.py:756

commit v3 on v2

--- a/solution.py
+++ b/solution.py
@@ -1,4 +1,5 @@
 import functools
+import heapq
 import math
 
 import jax
@@ -63,13 +64,32 @@
     return barrier, n_dom + n_rows - 2
 
 
+def wave_order(first):
+    chunks = len(first)
+    track = ["c", "y", "x", "z", "x", "y", "c"]
+    load = [1.5, 6.5, 2.0, 6.5, 2.0, 6.5, 1.5]
+    lag = [0.8, 1.8, 1.8, 3.5, 1.8, 1.8, 0.8]
+    free = {name: 0.0 for name in track}
+    ready = [(start, ch, 0) for ch, start in enumerate(first)]
+    heapq.heapify(ready)
+    order = []
+    while ready:
+        now, ch, stage = heapq.heappop(ready)
+        order.append((stage, ch))
+        if stage + 1 < len(track):
+            begin = max(now, free[track[stage]])
+            free[track[stage]] = begin + load[stage] / chunks
+            heapq.heappush(ready, (free[track[stage]] + lag[stage], ch, stage + 1))
+    return order
+
+
 def whole_kernel(
     sizes,
-    feat,
-    out_grad,
-    w_query,
-    w_keyval,
-    w_out,
+    feat_in,
+    out_grad_in,
+    w_query_in,
+    w_keyval_in,
+    w_out_in,
     virt,
     local_nbr,
     expander,
@@ -77,6 +97,11 @@
     grad_feat,
     total,
     virt_total,
+    feat,
+    out_grad,
+    w_query,
+    w_keyval,
+    w_out,
     picker,
     picked,
     slots,
@@ -84,7 +109,8 @@
     virt_pad,
     wkv_t,
     ext_t,
-    slot_t,
+    edge_x,
+    edge_x_sum,
     q_t,
     d_t,
     kv_t,
@@ -100,7 +126,7 @@
     out_t,
     dq_t,
     edge_grad,
-    slot_grad,
+    edge_feat,
     slot_feat,
     halo_feat,
     slots_back,
@@ -120,6 +146,7 @@
     virt_y,
     virt_x,
     virt_z,
+    sems_in,
     sems_s,
     sems_g,
     sems_a,
@@ -152,6 +179,20 @@
     span = per_group * per_peer
 
     barrier, arrivals = greet(n_dom, n_rows)
+    loads = [
+        pltpu.make_async_copy(src, dst, sems_in.at[i])
+        for i, (src, dst) in enumerate(
+            [
+                (feat_in, feat),
+                (w_keyval_in, w_keyval),
+                (w_query_in, w_query),
+                (w_out_in, w_out),
+                (out_grad_in, out_grad),
+            ]
+        )
+    ]
+    for load in loads:
+        load.start()
 
     spot = lax.broadcasted_iota(jnp.int32, (per_peer, slot_count), 1)
     entry = lax.broadcasted_iota(jnp.int32, (per_peer, slot_count), 0)
@@ -163,6 +204,7 @@
     send_flat = jnp.sum(jnp.where(mine, listed, 0.0), axis=0, keepdims=True).astype(jnp.int32)
     rows_at = lax.broadcasted_iota(jnp.int32, (row_count, slot_count), 0)
     picker[...] = (rows_at == send_flat).astype(F32).astype(BF16)
+    loads[0].wait()
     picked[...] = contract(picker[...], feat[...], 0, 0).astype(BF16).reshape(picked.shape)
 
     pl.semaphore_wait(barrier, arrivals)
@@ -194,6 +236,8 @@
     lax.fori_loop(1, n_dom, spread_start, 0)
     slots[0] = picked[dom]
 
+    for load in loads[1:]:
+        load.wait()
     wkv_t[...] = w_keyval[...].T
     ext_t[:, TILE:] = feat[...].T
     q_t[...] = contract(w_query[...], ext_t[:, TILE:], 0, 0).astype(BF16)
@@ -257,13 +301,16 @@
     for g in range(groups):
         lax.fori_loop(max(1, g * per_group), (g + 1) * per_group, spread_wait, 0)
         held = slice(g * span, (g + 1) * span)
-        slot_t[:, held] = slots[g * per_group : (g + 1) * per_group].reshape(span, width).T
-        slot_kv = contract(wkv_t[...], slot_t[:, held], 1, 0).astype(BF16)
-        chosen = contract(slot_kv, named[held, :], 1, 0)
+        found = contract(
+            slots[g * per_group : (g + 1) * per_group].reshape(span, width), named[held, :], 0, 0
+        )
         if g == 0:
-            edge_kv[...] = chosen
+            edge_x_sum[...] = found
+        elif g + 1 < groups:
+            edge_x_sum[...] += found
         else:
-            edge_kv[...] += chosen
+            edge_x[...] = (edge_x_sum[...] + found).astype(BF16)
+    edge_kv[...] = contract(wkv_t[...], edge_x[...], 1, 0).astype(BF16).astype(F32)
 
     q_wide = q_t[...].astype(F32)
     d_wide = d_t[...].astype(F32)
@@ -327,15 +374,16 @@
         back_copy(step).wait()
         return carry
 
-    for g in range(groups):
+    def slot_sums(g):
         held = slice(g * span, (g + 1) * span)
-        grad_g = contract(edge_grad[...], named[held, :], 1, 1).astype(BF16)
-        slot_grad[:, held] = grad_g
         slot_feat[g * per_group : (g + 1) * per_group] = (
-            contract(grad_g, w_keyval[...], 0, 1).astype(BF16).reshape(per_group, per_peer, width)
-        )
+            contract(named[held, :], edge_feat[...], 1, 1)
+            .astype(BF16)
+            .reshape(per_group, per_peer, width)
+        )
+
+    def slot_return(g):
         lax.fori_loop(max(1, g * per_group), (g + 1) * per_group, back_start, 0)
-    slots_back[dom] = slot_feat[0]
 
     kv_grad[...] = jnp.zeros_like(kv_grad)
     for h in range(HEADS):
@@ -590,7 +638,7 @@
     virt_lo = (virt_t - virt_hi.astype(F32)).astype(BF16)
     kv_sum = (
         contract(ext_t[...], kv_grad[...].astype(BF16), 1, 1)
-        + contract(slot_t[...], slot_grad[...], 1, 1)
+        + contract(edge_x[...], edge_grad[...], 1, 1)
         + contract(virt_b, virt_hi[:, 0:VROWS], 0, 1)
         + contract(virt_b, virt_lo[:, 0:VROWS], 0, 1)
     ).astype(BF16)
@@ -612,19 +660,27 @@
         lax.rem(row + n_rows - 1, n_rows),
     )
     halo_return.start()
-    stage_y(0)
-    stage_y(1)
-    stage_y(2)
-    grad_t = contract(w_query[...], dq_b, 1, 0) + contract(
-        w_keyval[...], kv_grad[:, TILE:].astype(BF16), 1, 0
-    )
-    grad_feat[...] = grad_t.T
-    for diagonal in range(2, len(stages) + chunks):
-        for ch in range(chunks):
-            stage = diagonal - ch
-            if 2 <= stage < len(stages):
-                stages[stage](ch)
-        virt_stage(diagonal - 1)
+    edge_feat[...] = contract(w_keyval[...], edge_grad[...], 1, 0).astype(BF16)
+    last = chunks - 1
+    for stage, ch in wave_order([0.0] + [1.5] * last):
+        if stage > 0:
+            stages[stage](ch)
+        if ch == last and 1 <= stage <= 4:
+            virt_stage(stage)
+        if (stage, ch) == (1, last):
+            for g in range(groups // 2):
+                slot_sums(g)
+                slot_return(g)
+            for g in range(groups // 2, groups):
+                slot_sums(g)
+            slots_back[dom] = slot_feat[0]
+            grad_t = contract(w_query[...], dq_b, 1, 0) + contract(
+                w_keyval[...], kv_grad[:, TILE:].astype(BF16), 1, 0
+            )
+            grad_feat[...] = grad_t.T
+        if (stage, ch) == (3, last):
+            for g in range(groups // 2, groups):
+                slot_return(g)
     halo_return.wait()
     lax.fori_loop(1, n_dom, back_wait, 0)
     summed = grad_feat[...] + contract(
@@ -636,17 +692,28 @@
         finish(("gc", ch))
 
 
-def finish_kernel(factor, go_in, gq_in, gk_in, gv_in, virt_in, feat_in, gq, gkv, go, gv, gf):
-    width = gq.shape[1]
-    gq[...] = gq_in[...].astype(F32) * factor
-    go[...] = go_in[...].astype(F32) * factor
-    gkv[:, 0:width] = gk_in[...].astype(F32) * factor
-    gkv[:, width:] = gv_in[...].astype(F32) * factor
-
-    @pl.when(pl.program_id(0) == 0)
-    def _():
-        gv[...] = virt_in[0 : gv.shape[0]] * factor
-        gf[...] = feat_in[...]
+def finish_kernel(
+    factor, total, virt_in, feat_in, gq, gkv, go, gv, gf, gq_v, gkv_v, go_v, gv_v, sems
+):
+    width = gq_v.shape[1]
+    copies = [
+        pltpu.make_async_copy(src, dst, sems.at[i])
+        for i, (src, dst) in enumerate(
+            [(feat_in, gf), (go_v, go), (gq_v, gq), (gkv_v, gkv), (gv_v, gv)]
+        )
+    ]
+    copies[0].start()
+    go_v[...] = total[0:width].astype(F32) * factor
+    copies[1].start()
+    gq_v[...] = total[width : 2 * width].astype(F32) * factor
+    copies[2].start()
+    gkv_v[:, 0:width] = total[2 * width : 3 * width].astype(F32) * factor
+    gkv_v[:, width:] = total[3 * width :].astype(F32) * factor
+    copies[3].start()
+    gv_v[...] = virt_in[0 : gv_v.shape[0]] * factor
+    copies[4].start()
+    for copy in copies:
+        copy.wait()
 
 
 def shards(sizes, features, out_grad, w_query, w_keyval, w_out, virtual, local_nbr, expander, send_rows):
@@ -670,9 +737,14 @@
             shape((chunks, height, width), BF16),
             shape((8, width), F32),
         ),
-        in_specs=[VMEM] * 9,
+        in_specs=[pl.BlockSpec(memory_space=pl.ANY)] * 5 + [VMEM] * 4,
         out_specs=(VMEM,) * 3,
         scratch_shapes=[
+            pltpu.VMEM((rows, width), BF16),
+            pltpu.VMEM((rows, width), BF16),
+            pltpu.VMEM((width, width), BF16),
+            pltpu.VMEM((width, 2 * width), BF16),
+            pltpu.VMEM((width, width), BF16),
             pltpu.VMEM((rows, slots), BF16),
             pltpu.VMEM((n_dom, per_peer, width), BF16),
             pltpu.VMEM((n_dom, per_peer, width), BF16),
@@ -680,7 +752,8 @@
             pltpu.VMEM((VROWS, width), F32),
             pltpu.VMEM((2 * width, width), BF16),
             pltpu.VMEM((width, rows + TILE), BF16),
-            pltpu.VMEM((width, slots), BF16),
+            pltpu.VMEM((width, 4 * rows), BF16),
+            pltpu.VMEM((width, 4 * rows), F32),
             pltpu.VMEM((width, rows), BF16),
             pltpu.VMEM((width, rows), BF16),
             pltpu.VMEM((2 * width, rows + TILE), BF16),
@@ -696,7 +769,7 @@
             pltpu.VMEM((width, rows), F32),
             pltpu.VMEM((width, rows), F32),
             pltpu.VMEM((2 * width, 4 * rows), BF16),
-            pltpu.VMEM((2 * width, slots), BF16),
+            pltpu.VMEM((width, 4 * rows), BF16),
             pltpu.VMEM((n_dom, per_peer, width), BF16),
             pltpu.VMEM((TILE, width), BF16),
             pltpu.VMEM((n_dom, per_peer, width), BF16),
@@ -716,6 +789,7 @@
             pltpu.VMEM((ny, 8, width), F32),
             pltpu.VMEM((nx, 8, width), F32),
             pltpu.VMEM((nz, 8, width), F32),
+            dma((5,)),
             dma((2, n_dom)),
             dma((2, n_dom)),
             dma((2,)),
@@ -744,19 +818,10 @@
         send_rows,
     )
 
-    flat = total.reshape(chunks * height, width)
-    steps = width // LANES
-
-    def rows_of(part):
-        return pl.BlockSpec((LANES, width), lambda i: (part * steps + i, 0))
-
-    def fixed(count):
-        return pl.BlockSpec((count, width), lambda i: (0, 0))
-
+    anywhere = pl.BlockSpec(memory_space=pl.ANY)
     gq, gkv, go, gv, gf = pl.pallas_call(
         functools.partial(finish_kernel, (rows * n_dom * n_rows) ** (-0.5)),
         name="finish",
-        grid=(steps,),
         out_shape=(
             shape((width, width), F32),
             shape((width, 2 * width), F32),
@@ -764,15 +829,16 @@
             shape((virtual.shape[0], width), F32),
             shape((rows, width), F32),
         ),
-        in_specs=[rows_of(0), rows_of(1), rows_of(2), rows_of(3), fixed(8), fixed(rows)],
-        out_specs=(
-            rows_of(0),
-            pl.BlockSpec((LANES, 2 * width), lambda i: (i, 0)),
-            rows_of(0),
-            fixed(virtual.shape[0]),
-            fixed(rows),
-        ),
-    )(flat, flat, flat, flat, virt_total, grad_feat)
+        in_specs=[VMEM] * 3,
+        out_specs=(anywhere,) * 5,
+        scratch_shapes=[
+            pltpu.VMEM((width, width), F32),
+            pltpu.VMEM((width, 2 * width), F32),
+            pltpu.VMEM((width, width), F32),
+            pltpu.VMEM((virtual.shape[0], width), F32),
+            dma((5,)),
+        ],
+    )(total.reshape(chunks * height, width), virt_total, grad_feat)
     return gf, gq, gkv, go, gv
 
 

time: 92 us -> 80.7 us (0.88)
  Pallas kernels: 91 us -> 79.8 us
    pallas_call x1, Pallas kernels: 87 us -> 76.9 us  [shards(): pl.pallas_call(functools.partial(whole_kernel, sizes), name='whole', out_...]
    pallas_call x1, Pallas kernels: 3.97 us -> 2.94 us  [shards(): pl.pallas_call(functools.partial(finish_kernel, (rows * n_dom * n_rows) *...]
where the time goes in v3:
time: 80.7 us; the launch traced here: 80.5 us
  Pallas kernels  79.8 us (99%)
    pallas_call x1, Pallas kernels, shards(): pl.pallas_call(functools.partial(whole_kernel, sizes), name='whole', out_...  76.9 us
    pallas_call x1, Pallas kernels, shards(): pl.pallas_call(functools.partial(finish_kernel, (rows * n_dom * n_rows) *...  2.94 us

profile of v3, /device:TPU:1, one launch (start us, length us, event | category | flops | bytes accessed | tf_op | source)
XLA Modules:
  0.0 80.5 jit_solution(13440894224958803078)
XLA Ops:
  0.6 76.9 %whole.1 = (f32[256,384]{1,0:T(8,128)}, bf16[3,512,384]{2,1,0:T(8,128)(2,1)}, f32[8,384]{1,0:T(8,128)}) custom-call(bf16[256,384]{1,0:T(8,128)(2,1)} %feat_in.1, bf16[256,384]{1,0:T(8,128)(2,1)} %out_grad_in.1, bf16[384,384]{1,0:T(8,128)(2,1)} %w_query_in.1, bf16[384,768]{1,0:T(8,128)(2,1)} %w_keyval_in.1, bf16[384,384]{1,0:T(8,128)(2,1)} %w_out_in.1, ...), custom_call_target="tpu_custom_call" | custom-call | tf_op jit(solution)/shard_map/whole/pallas_call | solution.py:732
  77.5 2.9 %finish.1 = (f32[384,384]{1,0:T(8,128)}, f32[384,768]{1,0:T(8,128)}, f32[384,384]{1,0:T(8,128)}, f32[4,384]{1,0:T(4,128)}, f32[256,384]{1,0:T(8,128)}) custom-call(bf16[1536,384]{1,0:T(8,128)(2,1)} %bitcast.3, f32[8,384]{1,0:T(8,128)} %get-tuple-element.14.virt_in, f32[256,384]{1,0:T(8,128)} %get-tuple-element.15.feat_in), custom_call_target="tpu_custom_call" | custom-call | tf_op jit(solution)/shard_map/finish/pallas_call | solution.py:822

commit v4 on v3

--- a/solution.py
+++ b/solution.py
@@ -66,9 +66,9 @@
 
 def wave_order(first):
     chunks = len(first)
-    track = ["c", "y", "x", "z", "x", "y", "c"]
-    load = [1.5, 6.5, 2.0, 6.5, 2.0, 6.5, 1.5]
-    lag = [0.8, 1.8, 1.8, 3.5, 1.8, 1.8, 0.8]
+    track = ["c", "y", "x", "z", "y", "c"]
+    load = [1.5, 6.5, 2.0, 6.5, 6.5, 1.5]
+    lag = [1.0, 2.5, 2.5, 4.0, 4.0, 1.0]
     free = {name: 0.0 for name in track}
     ready = [(start, ch, 0) for ch, start in enumerate(first)]
     heapq.heapify(ready)
@@ -139,8 +139,7 @@
     got_x,
     sum_x,
     got_z,
-    all_x,
-    all_y,
+    all_p,
     virt_feat,
     virt_c,
     virt_y,
@@ -155,8 +154,7 @@
     sems_y,
     sems_x,
     sems_z,
-    sems_gx,
-    sems_gy,
+    sems_gp,
     sems_gc,
     sems_v,
 ):
@@ -174,9 +172,18 @@
     scale = 1.0 / math.sqrt(head_dim)
     tiles = row_count // TILE
     bits = per_peer.bit_length() - 1
-    groups = 4
-    per_group = n_dom // groups
+    groups = nx
+    per_group = nz
     span = per_group * per_peer
+
+    def distance(offset, size):
+        return min(offset, size - offset)
+
+    far_groups = sorted(range(groups), key=lambda dx: -distance(dx, nx))
+    far_first = sorted(
+        [(dx, dz) for dx in range(nx) for dz in range(nz)][1:],
+        key=lambda offset: -distance(offset[0], nx) - distance(offset[1], nz),
+    )
 
     barrier, arrivals = greet(n_dom, n_rows)
     loads = [
@@ -219,21 +226,15 @@
     )
     halo_copy.start()
 
-    def spread_copy(step):
-        peer = lax.rem(dom + step, n_dom)
+    def spread_copy(dx, dz):
+        peer = lax.rem(x + dx, nx) * nz + lax.rem(z + dz, nz)
+        step = dx * nz + dz
         return remote(
             picked.at[peer], slots.at[step], sems_s.at[0, step], sems_s.at[1, step], peer, row
         )
 
-    def spread_start(step, carry):
-        spread_copy(step).start()
-        return carry
-
-    def spread_wait(step, carry):
-        spread_copy(step).wait()
-        return carry
-
-    lax.fori_loop(1, n_dom, spread_start, 0)
+    for dx, dz in far_first:
+        spread_copy(dx, dz).start()
     slots[0] = picked[dom]
 
     for load in loads[1:]:
@@ -255,8 +256,9 @@
     bias[...] = jnp.where(mask, 0.0, NEGATIVE_FILL)
 
     source = jnp.right_shift(expander[...], bits)
-    away = dom - source
-    away = jnp.where(away < 0, away + n_dom, away)
+    away_x = jnp.bitwise_and(x - jnp.right_shift(source, nz.bit_length() - 1), nx - 1)
+    away_z = jnp.bitwise_and(z - jnp.bitwise_and(source, nz - 1), nz - 1)
+    away = away_x * nz + away_z
     slot_of = away * per_peer + jnp.bitwise_and(expander[...], per_peer - 1)
     slot_ids = lax.broadcasted_iota(jnp.int32, (slot_count, row_count), 0)
     for k in range(degree):
@@ -298,15 +300,17 @@
             rows_f[h : h + 1, here] = jnp.sum(e, axis=0, keepdims=True)
             rows_d[h : h + 1, here] = jnp.sum(e * dp, axis=0, keepdims=True)
 
-    for g in range(groups):
-        lax.fori_loop(max(1, g * per_group), (g + 1) * per_group, spread_wait, 0)
+    for turn, g in enumerate(far_groups):
+        for dx, dz in far_first:
+            if dx == g:
+                spread_copy(dx, dz).wait()
         held = slice(g * span, (g + 1) * span)
         found = contract(
             slots[g * per_group : (g + 1) * per_group].reshape(span, width), named[held, :], 0, 0
         )
-        if g == 0:
+        if turn == 0:
             edge_x_sum[...] = found
-        elif g + 1 < groups:
+        elif turn + 1 < groups:
             edge_x_sum[...] += found
         else:
             edge_x[...] = (edge_x_sum[...] + found).astype(BF16)
@@ -355,8 +359,9 @@
     out_t[...] = out_sum
     dq_t[...] = dq_sum
 
-    def back_copy(step):
-        peer = lax.rem(dom - step + n_dom, n_dom)
+    def back_copy(dx, dz):
+        peer = lax.rem(x - dx + nx, nx) * nz + lax.rem(z - dz + nz, nz)
+        step = dx * nz + dz
         return remote(
             slot_feat.at[step],
             slots_back.at[dom],
@@ -366,14 +371,6 @@
             row,
         )
 
-    def back_start(step, carry):
-        back_copy(step).start()
-        return carry
-
-    def back_wait(step, carry):
-        back_copy(step).wait()
-        return carry
-
     def slot_sums(g):
         held = slice(g * span, (g + 1) * span)
         slot_feat[g * per_group : (g + 1) * per_group] = (
@@ -383,8 +380,14 @@
         )
 
     def slot_return(g):
-        lax.fori_loop(max(1, g * per_group), (g + 1) * per_group, back_start, 0)
-
+        for dx, dz in far_first:
+            if dx == g:
+                back_copy(dx, dz).start()
+
+    edge_feat[...] = contract(w_keyval[...], edge_grad[...], 1, 0).astype(BF16)
+    for g in far_groups[: groups // 2]:
+        slot_sums(g)
+        slot_return(g)
     kv_grad[...] = jnp.zeros_like(kv_grad)
     for h in range(HEADS):
         for t in range(tiles):
@@ -466,6 +469,11 @@
                 )
             ],
         )
+
+    plane = [(dx, dy) for dx in range(nx) for dy in range(ny)][1:]
+
+    def plane_peer(dx, dy):
+        return x_peer(dx) * nz + z, y_peer(dy) * 2 + core
 
     def stage_y(ch):
         finish(("c", ch))
@@ -528,52 +536,34 @@
         )
         got_z[ch, z] = acc.astype(BF16)
 
-    def stage_all_x(ch):
+    def stage_all_plane(ch):
         finish(("z", ch))
         acc = got_z[ch, 0].astype(F32)
         for s in range(1, nz):
             acc = acc + got_z[ch, s].astype(F32)
-        all_x[ch, block(x, piece)] = acc.astype(BF16)
+        mine = block(y * nx + x, piece)
+        all_p[ch, mine] = acc.astype(BF16)
         start(
-            ("gx", ch),
+            ("gp", ch),
             [
                 remote(
-                    all_x.at[ch, block(x, piece)],
-                    all_x.at[ch, block(x, piece)],
-                    sems_gx.at[0, ch, s],
-                    sems_gx.at[1, ch, s],
-                    x_peer(s) * nz + z,
-                    row,
+                    all_p.at[ch, mine],
+                    all_p.at[ch, mine],
+                    sems_gp.at[0, ch, i],
+                    sems_gp.at[1, ch, i],
+                    *plane_peer(dx, dy),
                 )
-                for s in range(1, nx)
+                for i, (dx, dy) in enumerate(plane)
             ],
         )
 
-    def stage_all_y(ch):
-        finish(("gx", ch))
-        start(
-            ("gy", ch),
-            [
-                remote(
-                    all_x.at[ch],
-                    all_y.at[ch, block(y, quarter)],
-                    sems_gy.at[0, ch, s],
-                    sems_gy.at[1, ch, s],
-                    dom,
-                    y_peer(s) * 2 + core,
-                )
-                for s in range(1, ny)
-            ],
-        )
-        all_y[ch, block(y, quarter)] = all_x[ch]
-
     def stage_all_c(ch):
-        finish(("gy", ch))
+        finish(("gp", ch))
         start(
             ("gc", ch),
             [
                 remote(
-                    all_y.at[ch],
+                    all_p.at[ch],
                     total.at[ch, block(core, half)],
                     sems_gc.at[0, ch],
                     sems_gc.at[1, ch],
@@ -582,7 +572,7 @@
                 )
             ],
         )
-        total[ch, block(core, half)] = all_y[ch]
+        total[ch, block(core, half)] = all_p[ch]
 
     def virt_exchange(key, buffer, index, first, peers):
         start(
@@ -629,7 +619,7 @@
         elif stage == 4:
             virt_total[...] = virt_sum("vz", virt_z)
 
-    stages = [stage_c, stage_y, stage_x, stage_z, stage_all_x, stage_all_y, stage_all_c]
+    stages = [stage_c, stage_y, stage_x, stage_z, stage_all_plane, stage_all_c]
 
     put(0, contract(out_b, out_grad[...], 1, 0).astype(BF16))
     put(1, contract(ext_t[:, TILE:], dq_b, 1, 1).astype(BF16))
@@ -646,48 +636,48 @@
     put(3, kv_sum[:, width:])
     stage_c(1)
     stage_c(2)
-    virt_feat[...] = (
-        contract(virt_hi, w_keyval[...], 0, 1) + contract(virt_lo, w_keyval[...], 0, 1)
-    )[0:8]
-    virt_stage(0)
-    halo_feat[...] = contract(kv_grad[:, 0:TILE].astype(BF16), w_keyval[...], 0, 1).astype(BF16)
-    halo_return = remote(
-        halo_feat,
-        halo_back,
-        sems_a.at[0],
-        sems_a.at[1],
-        dom,
-        lax.rem(row + n_rows - 1, n_rows),
-    )
-    halo_return.start()
-    edge_feat[...] = contract(w_keyval[...], edge_grad[...], 1, 0).astype(BF16)
     last = chunks - 1
+    virt_at = {(2, last): 1, (3, last): 2, (4, last): 3}
     for stage, ch in wave_order([0.0] + [1.5] * last):
         if stage > 0:
             stages[stage](ch)
-        if ch == last and 1 <= stage <= 4:
-            virt_stage(stage)
+        if (stage, ch) in virt_at:
+            virt_stage(virt_at[(stage, ch)])
         if (stage, ch) == (1, last):
-            for g in range(groups // 2):
+            virt_feat[...] = (
+                contract(virt_hi, w_keyval[...], 0, 1) + contract(virt_lo, w_keyval[...], 0, 1)
+            )[0:8]
+            virt_stage(0)
+            halo_feat[...] = contract(
+                kv_grad[:, 0:TILE].astype(BF16), w_keyval[...], 0, 1
+            ).astype(BF16)
+            halo_return = remote(
+                halo_feat,
+                halo_back,
+                sems_a.at[0],
+                sems_a.at[1],
+                dom,
+                lax.rem(row + n_rows - 1, n_rows),
+            )
+            halo_return.start()
+        if (stage, ch) == (3, last):
+            for g in far_groups[groups // 2 :]:
                 slot_sums(g)
                 slot_return(g)
-            for g in range(groups // 2, groups):
-                slot_sums(g)
             slots_back[dom] = slot_feat[0]
             grad_t = contract(w_query[...], dq_b, 1, 0) + contract(
                 w_keyval[...], kv_grad[:, TILE:].astype(BF16), 1, 0
             )
             grad_feat[...] = grad_t.T
-        if (stage, ch) == (3, last):
-            for g in range(groups // 2, groups):
-                slot_return(g)
     halo_return.wait()
-    lax.fori_loop(1, n_dom, back_wait, 0)
+    for dx, dz in far_first:
+        back_copy(dx, dz).wait()
     summed = grad_feat[...] + contract(
         picker[...], slots_back[...].reshape(slot_count, width), 1, 0
     )
     grad_feat[0 : row_count - TILE] = summed[0 : row_count - TILE]
     grad_feat[row_count - TILE :] = summed[row_count - TILE :] + halo_back[...].astype(F32)
+    virt_stage(4)
     for ch in range(chunks):
         finish(("gc", ch))
 
@@ -782,7 +772,6 @@
             pltpu.VMEM((chunks, nx - 1, piece, width), BF16),
             pltpu.VMEM((chunks, piece, width), BF16),
             pltpu.VMEM((chunks, nz, piece, width), BF16),
-            pltpu.VMEM((chunks, quarter, width), BF16),
             pltpu.VMEM((chunks, half, width), BF16),
             pltpu.VMEM((8, width), F32),
             pltpu.VMEM((2, 8, width), F32),
@@ -798,8 +787,7 @@
             dma((2, chunks, ny)),
             dma((2, chunks, nx)),
             dma((2, chunks, nz)),
-            dma((2, chunks, nx)),
-            dma((2, chunks, ny)),
+            dma((2, chunks, nx * ny)),
             dma((2, chunks)),
             dma((2, nx + ny + nz)),
         ],

time: 80.7 us -> 75 us (0.929)
  Pallas kernels: 79.8 us -> 74.1 us
    pallas_call x1, Pallas kernels: 76.9 us -> 71.2 us  [shards(): pl.pallas_call(functools.partial(whole_kernel, sizes), name='whole', out_...]
where the time goes in v4:
time: 75 us; the launch traced here: 74.7 us
  Pallas kernels  74.1 us (99%)
    pallas_call x1, Pallas kernels, shards(): pl.pallas_call(functools.partial(whole_kernel, sizes), name='whole', out_...  71.2 us
    pallas_call x1, Pallas kernels, shards(): pl.pallas_call(functools.partial(finish_kernel, (rows * n_dom * n_rows) *...  2.94 us

profile of v4, /device:TPU:1, one launch (start us, length us, event | category | flops | bytes accessed | tf_op | source)
XLA Modules:
  0.0 74.7 jit_solution(11557851616771060902)
XLA Ops:
  0.6 71.2 %whole.1 = (f32[256,384]{1,0:T(8,128)}, bf16[3,512,384]{2,1,0:T(8,128)(2,1)}, f32[8,384]{1,0:T(8,128)}) custom-call(bf16[256,384]{1,0:T(8,128)(2,1)} %feat_in.1, bf16[256,384]{1,0:T(8,128)(2,1)} %out_grad_in.1, bf16[384,384]{1,0:T(8,128)(2,1)} %w_query_in.1, bf16[384,768]{1,0:T(8,128)(2,1)} %w_keyval_in.1, bf16[384,384]{1,0:T(8,128)(2,1)} %w_out_in.1, ...), custom_call_target="tpu_custom_call" | custom-call | tf_op jit(solution)/shard_map/whole/pallas_call | solution.py:722
  71.8 2.9 %finish.1 = (f32[384,384]{1,0:T(8,128)}, f32[384,768]{1,0:T(8,128)}, f32[384,384]{1,0:T(8,128)}, f32[4,384]{1,0:T(4,128)}, f32[256,384]{1,0:T(8,128)}) custom-call(bf16[1536,384]{1,0:T(8,128)(2,1)} %bitcast.3, f32[8,384]{1,0:T(8,128)} %get-tuple-element.14.virt_in, f32[256,384]{1,0:T(8,128)} %get-tuple-element.15.feat_in), custom_call_target="tpu_custom_call" | custom-call | tf_op jit(solution)/shard_map/finish/pallas_call | solution.py:810
